TPU v7x, 32 devices: a whole 2x2x4 slice. The times are simulated.
32 devices in a mesh: mem: 4 (over x, core), row: 4 (over z), col: 2 (over y).
Axes of the slice: x: 2, y: 2, z: 4, core: 2. Of those that a mesh axis runs over, the one named last changes fastest.
Arguments:
- fields: bfloat16 [16, 16, 64, 256], P('mem', 'row', 'col'), may hold values from -6 to 6
- norm_gain: float32 [256], replicated, may hold values from 0.5 to 1.5
- w_query: bfloat16 [256, 256], replicated, may hold values from -11 to 11
- w_key: bfloat16 [256, 256], replicated, may hold values from -6 to 6
- w_value: bfloat16 [256, 256], replicated, may hold values from -0.375 to 0.375
- w_out: bfloat16 [256, 256], replicated, may hold values from -0.375 to 0.375
- mix_kernel: float32 [3, 3, 256], replicated, may hold values from -1.5 to 1.5
- cotangent: bfloat16 [16, 16, 64, 256], P('mem', 'row', 'col'), may hold values from -6 to 6
Outputs:
- grad_fields: bfloat16 [16, 16, 64, 256], P('mem', 'row', 'col')
- grad_gain: float32 [256], replicated
- grad_query: float32 [256, 256], replicated
- grad_key: float32 [256, 256], replicated
- grad_value: float32 [256, 256], replicated
- grad_out: float32 [256, 256], replicated
- grad_kernel: float32 [3, 3, 256], replicated
All inputs are finite; a program needn't handle non-finite values.
Results may differ from a plain program's by a relative error of at most 0.015.
The roundings to bfloat16 on the way count: a program that leaves them out, or rounds other values in their place, can miss the bound.
Values may be sent and summed in bfloat16 or wider, within the bound.
A program may use at most 64 MiB of HBM per device.

v0:
```python
import math

import jax
import jax.numpy as jnp
from jax import lax
from jax.sharding import PartitionSpec as P

HEADS = 8
CELLB = 64


epsilon = 1e-06


def with_halo(x, sides, width):
    for axis, dim in sides:
        size, length = (lax.axis_size(axis), x.shape[dim])
        up = [(i, (i + 1) % size) for i in range(size - 1)]
        down = [(j, i) for i, j in up]
        last = lax.slice_in_dim(x, length - width, length, axis=dim)
        first = lax.slice_in_dim(x, 0, width, axis=dim)
        before = lax.ppermute(last, axis, up)
        after = lax.ppermute(first, axis, down)
        x = jnp.concatenate([before, x, after], axis=dim)
    return x


def project(values, weight):
    shape = values.shape
    flat_in = values.reshape(-1, shape[-1])
    return jnp.dot(flat_in, weight, preferred_element_type=jnp.float32).reshape(
        shape[:-1] + (weight.shape[1],)
    )


def local(fields, norm_gain, w_query, w_key, w_value, w_out, mix_kernel, cotangent):
    members, tile_rows, tile_cols, model_width = fields.shape
    head_dim = model_width // HEADS
    score_scale = 1.0 / math.sqrt(head_dim)
    cell_count = tile_rows * tile_cols
    blocks = cell_count // CELLB
    padded_cot = with_halo(cotangent, (("row", 1), ("col", 2)), 1)
    summed = jnp.zeros(fields.shape, jnp.float32)
    for row_off in range(3):
        for col_off in range(3):
            summed = summed + mix_kernel[row_off, col_off] * padded_cot[
                :, 2 - row_off : 2 - row_off + tile_rows, 2 - col_off : 2 - col_off + tile_cols, :
            ].astype(jnp.float32)
    grad_mixed_all = summed.astype(jnp.bfloat16)

    def to_blocks(values):
        return jnp.swapaxes(values.reshape(members, blocks, CELLB, model_width), 0, 1)

    def one_block(running, block_in):
        blk_fields, blk_grad_mixed, blk_cot = block_in
        flat_in = blk_fields.astype(jnp.float32)
        inv_rms = lax.rsqrt(jnp.mean(flat_in * flat_in, axis=-1, keepdims=True) + epsilon)
        normed = flat_in * inv_rms
        inputs = (normed * norm_gain).astype(jnp.bfloat16)
        queries = project(inputs, w_query).astype(jnp.bfloat16)
        key_proj = project(inputs, w_key).astype(jnp.bfloat16)
        value_proj = project(inputs, w_value).astype(jnp.bfloat16)
        every_key, every_value = (
            lax.all_gather(key_proj, "mem", axis=0, tiled=True),
            lax.all_gather(value_proj, "mem", axis=0, tiled=True),
        )
        members_all = every_key.shape[0]
        local_shape = (members, CELLB, HEADS, head_dim)
        all_shape = (members_all, CELLB, HEADS, head_dim)
        query_heads = queries.reshape(local_shape)
        key_heads = every_key.reshape(all_shape)
        value_heads = every_value.reshape(all_shape)
        scores = (
            jnp.einsum(
                "mche,nche->chmn", query_heads, key_heads, preferred_element_type=jnp.float32
            )
            * score_scale
        )
        row_max = jnp.max(scores, axis=-1, keepdims=True)
        lifted = jnp.exp(scores - row_max)
        totals = jnp.sum(lifted, axis=-1, keepdims=True)
        attn_prob = lifted / totals
        prob_b = attn_prob.astype(jnp.bfloat16)
        attended = jnp.einsum(
            "chmn,nche->mche", prob_b, value_heads, preferred_element_type=jnp.float32
        ).astype(jnp.bfloat16)
        attended = attended.reshape(members, CELLB, model_width)
        mixed_blk = project(attended, w_out).astype(jnp.bfloat16)
        grad_att = project(blk_grad_mixed, w_out.T).astype(jnp.bfloat16)
        grad_heads = grad_att.reshape(local_shape)
        grad_prob = jnp.einsum(
            "mche,nche->chmn", grad_heads, value_heads, preferred_element_type=jnp.float32
        )
        inner = jnp.sum(attn_prob * grad_prob, axis=-1, keepdims=True)
        grad_score = (attn_prob * (grad_prob - inner) * score_scale).astype(jnp.bfloat16)
        grad_q = jnp.einsum(
            "chmn,nche->mche", grad_score, key_heads, preferred_element_type=jnp.float32
        ).astype(jnp.bfloat16)
        part_k = jnp.einsum(
            "chmn,mche->nche", grad_score, query_heads, preferred_element_type=jnp.float32
        ).reshape(members_all, CELLB, model_width)
        part_v = jnp.einsum(
            "chmn,mche->nche", prob_b, grad_heads, preferred_element_type=jnp.float32
        ).reshape(members_all, CELLB, model_width)
        sum_k, sum_v = (
            lax.psum_scatter(
                part_k.astype(jnp.bfloat16), "mem", scatter_dimension=0, tiled=True
            ).astype(jnp.float32),
            lax.psum_scatter(
                part_v.astype(jnp.bfloat16), "mem", scatter_dimension=0, tiled=True
            ).astype(jnp.float32),
        )
        flat_shape = (members * CELLB, model_width)
        grad_q2 = grad_q.reshape(flat_shape)
        grad_k2 = sum_k.astype(jnp.bfloat16).reshape(flat_shape)
        grad_v2 = sum_v.astype(jnp.bfloat16).reshape(flat_shape)
        inputs2 = inputs.reshape(flat_shape)
        grad_in = (
            jnp.dot(grad_q2, w_query.T, preferred_element_type=jnp.float32)
            + jnp.dot(grad_k2, w_key.T, preferred_element_type=jnp.float32)
            + jnp.dot(grad_v2, w_value.T, preferred_element_type=jnp.float32)
        )
        normed2 = normed.reshape(flat_shape)
        grad_normed = grad_in * norm_gain
        inv2 = inv_rms.reshape(-1, 1)
        grad_blk = blk_cot.reshape(flat_shape).astype(jnp.float32) + inv2 * (
            grad_normed - normed2 * jnp.mean(grad_normed * normed2, axis=-1, keepdims=True)
        )
        acc_q, acc_k, acc_v, acc_out, acc_gain = running
        acc_q = acc_q + jnp.einsum(
            "rd,re->de", inputs2, grad_q2, preferred_element_type=jnp.float32
        )
        acc_k = acc_k + jnp.einsum(
            "rd,re->de", inputs2, grad_k2, preferred_element_type=jnp.float32
        )
        acc_v = acc_v + jnp.einsum(
            "rd,re->de", inputs2, grad_v2, preferred_element_type=jnp.float32
        )
        acc_out = acc_out + jnp.einsum(
            "rd,re->de",
            attended.reshape(flat_shape),
            blk_grad_mixed.reshape(flat_shape),
            preferred_element_type=jnp.float32,
        )
        acc_gain = acc_gain + jnp.sum(grad_in * normed2, axis=0)
        outputs = (mixed_blk, grad_blk.astype(jnp.bfloat16).reshape(members, CELLB, model_width))
        return ((acc_q, acc_k, acc_v, acc_out, acc_gain), outputs)

    square = jnp.zeros((model_width, model_width), jnp.float32)
    start = (square, square, square, square, jnp.zeros((model_width,), jnp.float32))
    block_inputs = (to_blocks(fields), to_blocks(grad_mixed_all), to_blocks(cotangent))
    running, outputs = lax.scan(one_block, start, block_inputs)
    mixed_all = jnp.swapaxes(outputs[0], 0, 1).reshape(members, tile_rows, tile_cols, model_width)
    grad_fields = jnp.swapaxes(outputs[1], 0, 1).reshape(members, tile_rows, tile_cols, model_width)
    kernel_terms = []
    mixed_wide = mixed_all.astype(jnp.float32)
    for row_off in range(3):
        for col_off in range(3):
            shifted = padded_cot[
                :, 2 - row_off : 2 - row_off + tile_rows, 2 - col_off : 2 - col_off + tile_cols, :
            ].astype(jnp.float32)
            kernel_terms.append(jnp.sum(shifted * mixed_wide, axis=(0, 1, 2)))
    local_kernel = jnp.stack(kernel_terms).reshape(3, 3, model_width)
    acc_q, acc_k, acc_v, acc_out, acc_gain = running
    tot_q, tot_k, tot_v, tot_out, tot_gain, tot_kernel = lax.psum(
        (acc_q, acc_k, acc_v, acc_out, acc_gain, local_kernel), ("mem", "row", "col")
    )
    token_total = (
        members
        * lax.axis_size("mem")
        * tile_rows
        * lax.axis_size("row")
        * tile_cols
        * lax.axis_size("col")
    )
    scale_all = 1.0 / math.sqrt(token_total)
    return (
        grad_fields,
        tot_gain * scale_all,
        tot_q * scale_all,
        tot_k * scale_all,
        tot_v * scale_all,
        tot_out * scale_all,
        tot_kernel * scale_all,
    )


def solution(mesh):
    in_specs = (
        P("mem", "row", "col", None),
        P(),
        P(),
        P(),
        P(),
        P(),
        P(),
        P("mem", "row", "col", None),
    )
    out_specs = (P("mem", "row", "col", None), P(), P(), P(), P(), P(), P())
    return jax.shard_map(local, mesh=mesh, in_specs=in_specs, out_specs=out_specs, check_vma=False)
```

profile of v0, /device:TPU:0, one launch (start us, length us, event | category | flops | bytes accessed | tf_op | source)
XLA Modules:
  0.0 425.7 jit_solution(3508334397261388344)
XLA Ops:
  9.0 5.0 %collective-permute-start = (bf16[4,1,32,256]{3,2,1,0:T(8,128)(2,1)S(1)}, bf16[4,1,32,256]{3,2,1,0:T(8,128)(2,1)S(1)}, u32[]{:S(2)}, u32[]{:S(2)}) collective-permute-start(bf16[4,1,32,256]{3,2,1,0:T(8,128)(2,1)S(1)} %get-tuple-element.264), channel_id=1, source_target_pairs={{0,2},{2,4},{4,6},{1,3},{3,5},{5,7},{8,10},{10,12},{12,14},{9,11},... | collective-permute-start | bytes 196616 | tf_op jit(solution)/shard_map/ppermute | solution.py:22
  16.9 3.3 collective-permute-done.1
  21.5 4.5 %collective-permute-start.3 = (bf16[4,6,1,256]{3,2,1,0:T(2,128)(2,1)S(1)}, bf16[4,6,1,256]{3,2,1,0:T(2,128)(2,1)S(1)}, u32[]{:S(2)}, u32[]{:S(2)}) collective-permute-start(bf16[4,6,1,256]{3,2,1,0:T(2,128)(2,1)S(1)} %get-tuple-element.261), channel_id=1, source_target_pairs={{0,1},{2,3},{4,5},{6,7},{8,9},{10,11},{12,13},{14,15},{16,17},{18,... | collective-permute-start | bytes 36872 | tf_op jit(solution)/shard_map/ppermute | solution.py:22
  29.5 247.5 %while.23 = (s32[]{:T(128)}, f32[256,256]{1,0:T(8,128)}, f32[256,256]{1,0:T(8,128)}, f32[256,256]{1,0:T(8,128)}, f32[256,256]{1,0:T(8,128)}, /*index=5*/f32[256]...) while((s32[]{:T(128)}, f32[256,256]{1,0:T(8,128)}, ...), condition=%wide.region_9.10_spmd.clone, body=%wide.region_0.9_spmd.clone.sunk | while | flops 420385344 | bytes 48737236 | solution.py:152
  30.9 7.2 %all_gather.10 = bf16[16,64,256]{2,1,0:T(8,128)(2,1)S(1)} all-gather(bf16[4,64,256]{2,1,0:T(8,128)(2,1)S(1)} %convolution_convert_fusion.11), channel_id=1, replica_groups=mesh['mem'=4,'row'=4,'col'=2] {'mem'}, dimensions={0}, use_global_device_ids=true | all-gather | bytes 655360 | tf_op jit(solution)/shard_map/while/body/eval_jaxpr/all_gather | solution.py:64
  38.6 3.9 copy.127
  45.3 7.3 %all_gather.11 = bf16[16,64,256]{2,1,0:T(8,128)(2,1)S(1)} all-gather(bf16[4,64,256]{2,1,0:T(8,128)(2,1)S(1)} %convolution_convert_fusion.13), channel_id=1, replica_groups=mesh['mem'=4,'row'=4,'col'=2] {'mem'}, dimensions={0}, use_global_device_ids=true | all-gather | bytes 655360 | tf_op jit(solution)/shard_map/while/body/eval_jaxpr/all_gather | solution.py:65
  53.0 3.2 copy.131
  59.2 2.2 fusion.186
  61.4 5.1 %fusion.187 = (f32[64,8,4]{2,1,0:T(8,128)}, f32[64,8,4,16]{3,2,1,0:T(4,128)}) fusion(bf16[4,64,8,32]{3,0,2,1:T(4,128)(2,1)} %copy.133, bf16[16,64,8,32]{3,0,2,1:T(8,128)(2,1)} %copy.127), kind=kOutput, calls=%fused_computation.132.clone.1 | convolution fusion | flops 2195471 | bytes 794624 | tf_op jit(solution)/shard_map/while/body/eval_jaxpr/sub | solution.py:80
  66.5 26.8 %convert_bitcast_fusion.4 = bf16[16,64,8,32]{3,0,2,1:T(8,128)(2,1)} fusion(bf16[4,64,8,32]{3,0,2,1:T(4,128)(2,1)} %copy.133, f32[64,8,4,16]{3,2,1,0:T(4,128)S(1)} %fusion.186, f32[64,8,4,16]{3,2,1,0:T(4,128)} %get-tuple-element.383, f32[64,8,4]{2,1,0:T(8,128)} %get-tuple-element.384), kind=kOutput, calls=%fused_computation.3.clone.1 | convolution fusion | flops 2590735 | bytes 925696 | tf_op jit(solution)/shard_map/while/body/eval_jaxpr/chmn,mche->nche/dot_general | solution.py:99
  93.3 4.1 copy.135
  97.5 5.1 %convert_bitcast_fusion.5 = bf16[16,64,8,32]{3,0,2,1:T(8,128)(2,1)} fusion(bf16[4,64,8,32]{3,0,2,1:T(4,128)(2,1)S(1)} %copy-done.1, f32[64,8,4,16]{3,2,1,0:T(4,128)} %get-tuple-element.383, f32[64,8,4]{2,1,0:T(8,128)S(1)} %copy-done.34), kind=kOutput, calls=%fused_computation.2.clone.1 | convolution fusion | flops 2424832 | bytes 794624 | tf_op jit(solution)/shard_map/while/body/eval_jaxpr/chmn,mche->nche/dot_general | solution.py:102
  102.5 4.1 copy.136
  106.7 25.9 %fusion.188 = bf16[4,64,8,32]{3,0,2,1:T(4,128)(2,1)} fusion(bf16[16,64,8,32]{3,0,2,1:T(8,128)(2,1)} %copy.127, f32[64,8,4,16]{3,2,1,0:T(4,128)S(1)} %copy-done.3, f32[64,8,4,16]{3,2,1,0:T(4,128)} %get-tuple-element.383, f32[64,8,4]{2,1,0:T(8,128)} %get-tuple-element.384), kind=kOutput, calls=%fused_computation.13.clone.1 | convolution fusion | flops 2394127 | bytes 925696 | tf_op jit(solution)/shard_map/while/body/eval_jaxpr/chmn,nche->mche/dot_general | solution.py:96
  132.6 2.2 fusion.191
  142.9 7.4 %reduce-scatter.5.cloned.1.call-done = bf16[4,64,256]{1,2,0:T(8,128)(2,1)} async-done(((bf16[16,64,256]{1,2,0:T(8,128)(2,1)}), bf16[4,64,256]{1,2,0:T(8,128)(2,1)}) %reduce-scatter.5.cloned.1.call-update) | async-done | bytes 131088 | tf_op jit(solution)/shard_map/while/body/eval_jaxpr/reduce_scatter | solution.py:109
  154.9 6.6 %all_gather.10 = bf16[16,64,256]{2,1,0:T(8,128)(2,1)S(1)} all-gather(bf16[4,64,256]{2,1,0:T(8,128)(2,1)S(1)} %convolution_convert_fusion.11), channel_id=1, replica_groups=mesh['mem'=4,'row'=4,'col'=2] {'mem'}, dimensions={0}, use_global_device_ids=true | all-gather | bytes 655360 | tf_op jit(solution)/shard_map/while/body/eval_jaxpr/all_gather | solution.py:64
  162.0 3.9 copy.127
  168.7 7.3 %all_gather.11 = bf16[16,64,256]{2,1,0:T(8,128)(2,1)S(1)} all-gather(bf16[4,64,256]{2,1,0:T(8,128)(2,1)S(1)} %convolution_convert_fusion.13), channel_id=1, replica_groups=mesh['mem'=4,'row'=4,'col'=2] {'mem'}, dimensions={0}, use_global_device_ids=true | all-gather | bytes 655360 | tf_op jit(solution)/shard_map/while/body/eval_jaxpr/all_gather | solution.py:65
  176.5 3.2 copy.131
  182.6 2.2 fusion.186
  184.8 5.1 %fusion.187 = (f32[64,8,4]{2,1,0:T(8,128)}, f32[64,8,4,16]{3,2,1,0:T(4,128)}) fusion(bf16[4,64,8,32]{3,0,2,1:T(4,128)(2,1)} %copy.133, bf16[16,64,8,32]{3,0,2,1:T(8,128)(2,1)} %copy.127), kind=kOutput, calls=%fused_computation.132.clone.1 | convolution fusion | flops 2195471 | bytes 794624 | tf_op jit(solution)/shard_map/while/body/eval_jaxpr/sub | solution.py:80
  189.9 26.8 %convert_bitcast_fusion.4 = bf16[16,64,8,32]{3,0,2,1:T(8,128)(2,1)} fusion(bf16[4,64,8,32]{3,0,2,1:T(4,128)(2,1)} %copy.133, f32[64,8,4,16]{3,2,1,0:T(4,128)S(1)} %fusion.186, f32[64,8,4,16]{3,2,1,0:T(4,128)} %get-tuple-element.383, f32[64,8,4]{2,1,0:T(8,128)} %get-tuple-element.384), kind=kOutput, calls=%fused_computation.3.clone.1 | convolution fusion | flops 2590735 | bytes 925696 | tf_op jit(solution)/shard_map/while/body/eval_jaxpr/chmn,mche->nche/dot_general | solution.py:99
  216.7 4.1 copy.135
  220.9 5.1 %convert_bitcast_fusion.5 = bf16[16,64,8,32]{3,0,2,1:T(8,128)(2,1)} fusion(bf16[4,64,8,32]{3,0,2,1:T(4,128)(2,1)S(1)} %copy-done.1, f32[64,8,4,16]{3,2,1,0:T(4,128)} %get-tuple-element.383, f32[64,8,4]{2,1,0:T(8,128)S(1)} %copy-done.34), kind=kOutput, calls=%fused_computation.2.clone.1 | convolution fusion | flops 2424832 | bytes 794624 | tf_op jit(solution)/shard_map/while/body/eval_jaxpr/chmn,mche->nche/dot_general | solution.py:102
  226.0 4.2 copy.136
  230.2 25.9 %fusion.188 = bf16[4,64,8,32]{3,0,2,1:T(4,128)(2,1)} fusion(bf16[16,64,8,32]{3,0,2,1:T(8,128)(2,1)} %copy.127, f32[64,8,4,16]{3,2,1,0:T(4,128)S(1)} %copy-done.3, f32[64,8,4,16]{3,2,1,0:T(4,128)} %get-tuple-element.383, f32[64,8,4]{2,1,0:T(8,128)} %get-tuple-element.384), kind=kOutput, calls=%fused_computation.13.clone.1 | convolution fusion | flops 2394127 | bytes 925696 | tf_op jit(solution)/shard_map/while/body/eval_jaxpr/chmn,nche->mche/dot_general | solution.py:96
  256.1 2.2 fusion.191
  267.4 6.3 %reduce-scatter.5.cloned.1.call-done = bf16[4,64,256]{1,2,0:T(8,128)(2,1)} async-done(((bf16[16,64,256]{1,2,0:T(8,128)(2,1)}), bf16[4,64,256]{1,2,0:T(8,128)(2,1)}) %reduce-scatter.5.cloned.1.call-update) | async-done | bytes 131088 | tf_op jit(solution)/shard_map/while/body/eval_jaxpr/reduce_scatter | solution.py:109
  280.6 39.6 %all-reduce = (f32[256]{0:T(256)S(1)}, f32[3,3,256]{2,1,0:T(4,128)S(1)}) all-reduce(f32[256]{0:T(256)S(1)} %get-tuple-element.506, f32[3,3,256]{2,1,0:T(4,128)S(1)} %reshape.186), channel_id=1, replica_groups=mesh['mem'=4,'row'=4,'col'=2] {'mem','row','col'}, use_global_device_ids=true, to_apply=%region_10.11 | all-reduce | flops 2560 | bytes 20480 | tf_op jit(solution)/shard_map/psum | solution.py:165
  321.4 93.5 %all-reduce.4.cloned.1.call-done = (f32[256,256]{1,0:T(8,128)}, f32[256,256]{1,0:T(8,128)}, f32[256,256]{1,0:T(8,128)}, f32[256,256]{1,0:T(8,128)}) async-done(((f32[256,256]{1,0:T(8,128)}, f32[256,256]{1,0:T(8,128)}, f32[256,256]{1,0:T(8,128)}, f32[256,256]{1,0:T(8,128)}), (f32[256,256]{1,0:T(8,128)}, f32[256,256]{1,0:T(8,128)}, f32[256,256]{1,0:T(8,128)}, ...) | async-done | bytes 1048592 | tf_op jit(solution)/shard_map/psum | solution.py:165
  (224 shorter events, 56.0 us)
Async XLA Ops:
  8.0 21.5 %copy-start.16 = (bf16[4,4,32,256]{3,2,1,0:T(8,128)(2,1)S(1)}, bf16[4,4,32,256]{3,2,1,0:T(8,128)(2,1)}, u32[]{:S(2)}) copy-start(bf16[4,4,32,256]{3,2,1,0:T(8,128)(2,1)} %param.17) | copy-start | bytes 786436
  8.0 21.4 %copy-start = (bf16[4,4,32,256]{3,2,1,0:T(8,128)(2,1)S(1)}, bf16[4,4,32,256]{3,2,1,0:T(8,128)(2,1)}, u32[]{:S(2)}) copy-start(bf16[4,4,32,256]{3,2,1,0:T(8,128)(2,1)} %param.10) | copy-start | bytes 786436
  8.0 21.4 %copy-start.24 = (f32[256]{0:T(256)S(1)}, f32[256]{0:T(256)}, u32[]{:S(2)}) copy-start(f32[256]{0:T(256)} %param.11) | copy-start | bytes 3076
  8.0 21.4 %copy-start.6 = (bf16[256,256]{1,0:T(8,128)(2,1)S(1)}, bf16[256,256]{1,0:T(8,128)(2,1)}, u32[]{:S(2)}) copy-start(bf16[256,256]{1,0:T(8,128)(2,1)} %param.15) | copy-start | bytes 393220
  8.0 21.4 %copy-start.8 = (bf16[256,256]{1,0:T(8,128)(2,1)S(1)}, bf16[256,256]{1,0:T(8,128)(2,1)}, u32[]{:S(2)}) copy-start(bf16[256,256]{1,0:T(8,128)(2,1)} %param.14) | copy-start | bytes 393220
  9.0 6.9 %collective-permute-start = (bf16[4,1,32,256]{3,2,1,0:T(8,128)(2,1)S(1)}, bf16[4,1,32,256]{3,2,1,0:T(8,128)(2,1)S(1)}, u32[]{:S(2)}, u32[]{:S(2)}) collective-permute-start(bf16[4,1,32,256]{3,2,1,0:T(8,128)(2,1)S(1)} %get-tuple-element.264), channel_id=1, source_target_pairs={{0,2},{2,4},{4,6},{1,3},{3,5},{5,7},{8,10},{10,12},{12,14},{9,11},... | collective-permute-start | bytes 196616 | tf_op jit(solution)/shard_map/ppermute | solution.py:22
  14.0 6.2 %collective-permute-start.1 = (bf16[4,1,32,256]{3,2,1,0:T(8,128)(2,1)S(1)}, bf16[4,1,32,256]{3,2,1,0:T(8,128)(2,1)S(1)}, u32[]{:S(2)}, u32[]{:S(2)}) collective-permute-start(bf16[4,1,32,256]{3,2,1,0:T(8,128)(2,1)S(1)} %get-tuple-element.263), channel_id=1, source_target_pairs={{2,0},{4,2},{6,4},{3,1},{5,3},{7,5},{10,8},{12,10},{14,12},{11,9},... | collective-permute-start | bytes 196616 | tf_op jit(solution)/shard_map/ppermute | solution.py:23
  15.9 13.7 %copy-start.25 = (bf16[4,1,32,256]{3,2,1,0:T(8,128)(2,1)}, bf16[4,1,32,256]{3,2,1,0:T(8,128)(2,1)S(1)}, u32[]{:S(2)}) copy-start(bf16[4,1,32,256]{3,2,1,0:T(8,128)(2,1)S(1)} %collective-permute-done) | copy-start | bytes 196612
  20.2 6.8 %collective-permute-start.2 = (bf16[4,6,1,256]{3,2,1,0:T(2,128)(2,1)S(1)}, bf16[4,6,1,256]{3,2,1,0:T(2,128)(2,1)S(1)}, u32[]{:S(2)}, u32[]{:S(2)}) collective-permute-start(bf16[4,6,1,256]{3,2,1,0:T(2,128)(2,1)S(1)} %get-tuple-element.262), channel_id=1, source_target_pairs={{1,0},{3,2},{5,4},{7,6},{9,8},{11,10},{13,12},{15,14},{17,16},{19,... | collective-permute-start | bytes 36872 | tf_op jit(solution)/shard_map/ppermute | solution.py:23
  21.5 6.1 %collective-permute-start.3 = (bf16[4,6,1,256]{3,2,1,0:T(2,128)(2,1)S(1)}, bf16[4,6,1,256]{3,2,1,0:T(2,128)(2,1)S(1)}, u32[]{:S(2)}, u32[]{:S(2)}) collective-permute-start(bf16[4,6,1,256]{3,2,1,0:T(2,128)(2,1)S(1)} %get-tuple-element.261), channel_id=1, source_target_pairs={{0,1},{2,3},{4,5},{6,7},{8,9},{10,11},{12,13},{14,15},{16,17},{18,... | collective-permute-start | bytes 36872 | tf_op jit(solution)/shard_map/ppermute | solution.py:22
  29.6 12.9 %copy-start.20 = (bf16[2,4,64,256]{3,2,0,1:T(8,128)(2,1)}, bf16[2,4,64,256]{3,2,0,1:T(8,128)(2,1)S(1)}, u32[]{:S(2)}) copy-start(bf16[2,4,64,256]{3,2,0,1:T(8,128)(2,1)S(1)} %get-tuple-element.437) | copy-start | bytes 786436 | tf_op jit(solution)/shard_map/while
  29.6 111.0 %reduce-scatter.3.cloned.1.call-start = ((), (), s32[]{:S(2)}) async-start(), calls=%async_computation.3 | async-start | bytes 1310720 | tf_op jit(solution)/shard_map/while/body/eval_jaxpr/reduce_scatter | solution.py:106
  97.4 52.9 %reduce-scatter.5.cloned.1.call-start = ((), (), s32[]{:S(2)}) async-start(), calls=%async_computation.4 | async-start | bytes 1310720 | tf_op jit(solution)/shard_map/while/body/eval_jaxpr/reduce_scatter | solution.py:109
  138.4 13.0 %copy-start.9 = (bf16[256,256]{1,0:T(8,128)(2,1)S(1)}, bf16[256,256]{1,0:T(8,128)(2,1)}, u32[]{:S(2)}) copy-start(bf16[256,256]{1,0:T(8,128)(2,1)} %get-tuple-element.497) | copy-start | bytes 393220 | tf_op jit(solution)/shard_map/while
  139.0 12.8 %copy-start.10 = (bf16[1,4,64,256]{3,2,0,1:T(8,128)(2,1)S(1)}, bf16[1,4,64,256]{3,2,0,1:T(8,128)(2,1)}, u32[]{:S(2)}) copy-start(bf16[1,4,64,256]{3,2,0,1:T(8,128)(2,1)} %get-tuple-element.387) | copy-start | bytes 393220 | tf_op jit(solution)/shard_map/while
  139.2 12.7 %copy-start.29 = (bf16[2,4,64,256]{3,2,1,0:T(8,128)(2,1)S(1)}, bf16[2,4,64,256]{3,2,1,0:T(8,128)(2,1)}, u32[]{:S(2)}) copy-start(bf16[2,4,64,256]{3,2,1,0:T(8,128)(2,1)} %get-tuple-element.414) | copy-start | bytes 786436 | tf_op jit(solution)/shard_map/while
  139.6 12.3 %copy-start.12 = (f32[256,256]{1,0:T(8,128)S(1)}, f32[256,256]{1,0:T(8,128)}, u32[]{:S(2)}) copy-start(f32[256,256]{1,0:T(8,128)} %get-tuple-element.409) | copy-start | bytes 786436 | tf_op jit(solution)/shard_map/while
  140.5 11.9 %copy-start.14 = (f32[256,256]{1,0:T(8,128)S(1)}, f32[256,256]{1,0:T(8,128)}, u32[]{:S(2)}) copy-start(f32[256,256]{1,0:T(8,128)} %get-tuple-element.410) | copy-start | bytes 786436 | tf_op jit(solution)/shard_map/while
  140.5 11.4 %copy-start.4 = (bf16[4,64,256]{1,2,0:T(8,128)(2,1)S(1)}, bf16[4,64,256]{1,2,0:T(8,128)(2,1)}, u32[]{:S(2)}) copy-start(bf16[4,64,256]{1,2,0:T(8,128)(2,1)} %reduce-scatter.3.cloned.1.call-done) | copy-start | bytes 393220 | tf_op jit(solution)/shard_map/while
  142.8 10.7 %copy-start.17 = (bf16[4,4,32,256]{3,2,1,0:T(8,128)(2,1)S(1)}, bf16[4,4,32,256]{3,2,1,0:T(8,128)(2,1)}, u32[]{:S(2)}) copy-start(bf16[4,4,32,256]{3,2,1,0:T(8,128)(2,1)} %get-tuple-element.521) | copy-start | bytes 786436 | tf_op jit(solution)/shard_map/while
  142.9 10.7 %copy-start.21 = (bf16[2,4,64,256]{3,2,0,1:T(8,128)(2,1)S(1)}, bf16[2,4,64,256]{3,2,0,1:T(8,128)(2,1)}, u32[]{:S(2)}) copy-start(bf16[2,4,64,256]{3,2,0,1:T(8,128)(2,1)} %copy-done.20) | copy-start | bytes 786436 | tf_op jit(solution)/shard_map/while
  153.6 12.3 %copy-start.20 = (bf16[2,4,64,256]{3,2,0,1:T(8,128)(2,1)}, bf16[2,4,64,256]{3,2,0,1:T(8,128)(2,1)S(1)}, u32[]{:S(2)}) copy-start(bf16[2,4,64,256]{3,2,0,1:T(8,128)(2,1)S(1)} %get-tuple-element.437) | copy-start | bytes 786436 | tf_op jit(solution)/shard_map/while
  153.6 111.5 %reduce-scatter.3.cloned.1.call-start = ((), (), s32[]{:S(2)}) async-start(), calls=%async_computation.3 | async-start | bytes 1310720 | tf_op jit(solution)/shard_map/while/body/eval_jaxpr/reduce_scatter | solution.py:106
  220.8 52.9 %reduce-scatter.5.cloned.1.call-start = ((), (), s32[]{:S(2)}) async-start(), calls=%async_computation.4 | async-start | bytes 1310720 | tf_op jit(solution)/shard_map/while/body/eval_jaxpr/reduce_scatter | solution.py:109
  261.9 12.9 %copy-start.9 = (bf16[256,256]{1,0:T(8,128)(2,1)S(1)}, bf16[256,256]{1,0:T(8,128)(2,1)}, u32[]{:S(2)}) copy-start(bf16[256,256]{1,0:T(8,128)(2,1)} %get-tuple-element.497) | copy-start | bytes 393220 | tf_op jit(solution)/shard_map/while
  262.5 12.8 %copy-start.10 = (bf16[1,4,64,256]{3,2,0,1:T(8,128)(2,1)S(1)}, bf16[1,4,64,256]{3,2,0,1:T(8,128)(2,1)}, u32[]{:S(2)}) copy-start(bf16[1,4,64,256]{3,2,0,1:T(8,128)(2,1)} %get-tuple-element.387) | copy-start | bytes 393220 | tf_op jit(solution)/shard_map/while
  262.8 12.6 %copy-start.29 = (bf16[2,4,64,256]{3,2,1,0:T(8,128)(2,1)S(1)}, bf16[2,4,64,256]{3,2,1,0:T(8,128)(2,1)}, u32[]{:S(2)}) copy-start(bf16[2,4,64,256]{3,2,1,0:T(8,128)(2,1)} %get-tuple-element.414) | copy-start | bytes 786436 | tf_op jit(solution)/shard_map/while
  263.1 12.3 %copy-start.12 = (f32[256,256]{1,0:T(8,128)S(1)}, f32[256,256]{1,0:T(8,128)}, u32[]{:S(2)}) copy-start(f32[256,256]{1,0:T(8,128)} %get-tuple-element.409) | copy-start | bytes 786436 | tf_op jit(solution)/shard_map/while
  265.0 10.8 %copy-start.14 = (f32[256,256]{1,0:T(8,128)S(1)}, f32[256,256]{1,0:T(8,128)}, u32[]{:S(2)}) copy-start(f32[256,256]{1,0:T(8,128)} %get-tuple-element.410) | copy-start | bytes 786436 | tf_op jit(solution)/shard_map/while
  265.0 10.4 %copy-start.4 = (bf16[4,64,256]{1,2,0:T(8,128)(2,1)S(1)}, bf16[4,64,256]{1,2,0:T(8,128)(2,1)}, u32[]{:S(2)}) copy-start(bf16[4,64,256]{1,2,0:T(8,128)(2,1)} %reduce-scatter.3.cloned.1.call-done) | copy-start | bytes 393220 | tf_op jit(solution)/shard_map/while
  267.3 9.7 %copy-start.17 = (bf16[4,4,32,256]{3,2,1,0:T(8,128)(2,1)S(1)}, bf16[4,4,32,256]{3,2,1,0:T(8,128)(2,1)}, u32[]{:S(2)}) copy-start(bf16[4,4,32,256]{3,2,1,0:T(8,128)(2,1)} %get-tuple-element.521) | copy-start | bytes 786436 | tf_op jit(solution)/shard_map/while
  277.0 137.9 %all-reduce.4.cloned.1.call-start = ((), (), s32[]{:S(2)}) async-start(), calls=%async_computation.2 | async-start | bytes 2097152 | tf_op jit(solution)/shard_map/psum | solution.py:165
  (35 other events, 120.9 us)
Sparse Core Ops, SparseCore 0:
  97.5 25.1 reduce-scatter.2
  125.3 24.9 reduce-scatter.4
  220.9 25.3 reduce-scatter.2
  248.7 24.9 reduce-scatter.4
Sparse Core Ops, SparseCore 1:
  283.6 131.2 all-reduce.3
where the time goes:
time: 427 us; the launch traced here: 426 us
  matrix products  149 us (35%)
  waiting for transfers between devices  112 us (26%)
  blocking collectives  67.9 us (16%)
  local copies, waits for them, and re-layouts  58.4 us (14%)
  between operations  15.4 us (4%)
  starting transfers between devices  12.3 us (3%)
  other arithmetic  10.3 us (2%)
    psum x1, waiting for transfers between devices, local(): lax.psum((acc_q, acc_k, acc_v, acc_out, acc_gain, local_kernel), ('mem',...  93.5 us
    dot_general x2, matrix products, one_block(): jnp.einsum('chmn,mche->nche', grad_score, query_heads, preferred_element_...  53.6 us
    dot_general x2, matrix products, one_block(): jnp.einsum('chmn,nche->mche', grad_score, key_heads, preferred_element_ty...  51.7 us
    psum x1, blocking collectives, local(): lax.psum((acc_q, acc_k, acc_v, acc_out, acc_gain, local_kernel), ('mem',...  39.6 us
    all_gather x2, blocking collectives, one_block(): lax.all_gather(value_proj, 'mem', axis=0, tiled=True)  14.6 us
    all_gather x2, blocking collectives, one_block(): lax.all_gather(key_proj, 'mem', axis=0, tiled=True)  13.8 us
    reduce_scatter x2, waiting for transfers between devices, one_block(): lax.psum_scatter(part_v.astype(jnp.bfloat16), 'mem', scatter_dimension=0,...  13.7 us
    sub x2, matrix products, one_block(): lifted = jnp.exp(scores - row_max)  10.3 us
  transfers between devices with their start and end apart: 9, of which 6 were waited for; matrix products, arithmetic and copies ran while one was open for 23% of the time, Pallas kernels for 0%

commit v1 on v0

v1 whole, which is shorter than its diff:
```python
import functools
import math

import jax
import jax.numpy as jnp
from jax import lax
from jax.experimental import pallas as pl
from jax.experimental.pallas import tpu as pltpu
from jax.sharding import PartitionSpec as P

HEADS = 8
SUB = 8

epsilon = 1e-06
F32 = jnp.float32
BF16 = jnp.bfloat16


def dot_nn(a, b):
    return lax.dot_general(a, b, (((1,), (0,)), ((), ())), preferred_element_type=F32)


def dot_nt(a, b):
    return lax.dot_general(a, b, (((1,), (1,)), ((), ())), preferred_element_type=F32)


def flip(x):
    return x.astype(F32).T.astype(x.dtype)


def to_groups(x):
    members, cells, width = x.shape
    return jnp.concatenate(
        [x[:, i : i + SUB, :].reshape(members * SUB, width) for i in range(0, cells, SUB)], axis=0
    )


def from_groups(x, members, cells):
    width = x.shape[-1]
    size = members * SUB
    return jnp.concatenate(
        [x[g * size : (g + 1) * size].reshape(members, SUB, width) for g in range(cells // SUB)],
        axis=1,
    )


def attend_group(keys, vals, q_t, ga_t, k_t, v_t):
    tokens, width = keys.shape
    members = tokens // SUB
    head_dim = width // HEADS
    scale = 1.0 / math.sqrt(head_dim)
    head_of = lax.broadcasted_iota(jnp.int32, (tokens, width), 1) // head_dim
    row_cell = lax.broadcasted_iota(jnp.int32, (SUB, tokens), 0)
    col_cell = lax.broadcasted_iota(jnp.int32, (SUB, tokens), 1) % SUB
    same = (row_cell == col_cell)[None]
    outs = ([], [], [], [])
    for h in range(HEADS):
        own = head_of == h
        hs = slice(h * head_dim, (h + 1) * head_dim)
        k_own = jnp.where(own, keys.astype(F32), 0.0).astype(BF16)
        v_own = jnp.where(own, vals.astype(F32), 0.0).astype(BF16)
        scores = dot_nn(k_own, q_t).reshape(members, SUB, tokens) * scale
        grad_prob = dot_nn(v_own, ga_t).reshape(members, SUB, tokens)
        lifted = jnp.exp(scores - jnp.max(scores, axis=0, keepdims=True))
        prob = lifted * (1.0 / jnp.sum(lifted, axis=0, keepdims=True))
        inner = jnp.sum(prob * grad_prob, axis=0, keepdims=True)
        grad_score = prob * (grad_prob - inner) * scale
        prob_b = jnp.where(same, prob, 0.0).reshape(tokens, tokens).astype(BF16)
        gs_b = jnp.where(same, grad_score, 0.0).reshape(tokens, tokens).astype(BF16)
        outs[0].append(dot_nn(v_t[hs], prob_b))
        outs[1].append(dot_nn(k_t[hs], gs_b))
        outs[2].append(dot_nt(q_t[hs], gs_b))
        outs[3].append(dot_nt(ga_t[hs], prob_b))
    return tuple(jnp.concatenate(o, axis=0).astype(BF16) for o in outs)


def block_kernel(
    f_ref, gm_ref, gain_ref, wq_ref, wk_ref, wv_ref, wo_ref,
    corr_ref, mixed_ref, grads_ref, gain_out_ref,
):
    members, cells, width = f_ref.shape
    size = members * SUB
    flat = to_groups(f_ref[...].astype(F32))
    gm = to_groups(gm_ref[...].astype(F32)).astype(BF16)
    wq, wk, wv, wo = (w[...] for w in (wq_ref, wk_ref, wv_ref, wo_ref))
    inv = lax.rsqrt(jnp.mean(flat * flat, axis=-1, keepdims=True) + epsilon)
    normed = flat * inv
    inputs = (normed * gain_ref[...]).astype(BF16)
    in_t = flip(inputs)
    keys = dot_nn(inputs, wk).astype(BF16)
    vals = dot_nn(inputs, wv).astype(BF16)
    q_t = dot_nn(flip(wq), in_t).astype(BF16)
    k_t = dot_nn(flip(wk), in_t).astype(BF16)
    v_t = dot_nn(flip(wv), in_t).astype(BF16)
    ga_t = dot_nt(wo, gm).astype(BF16)
    parts = []
    for g in range(cells // SUB):
        rows = slice(g * size, (g + 1) * size)
        parts.append(
            attend_group(
                keys[rows], vals[rows], q_t[:, rows], ga_t[:, rows], k_t[:, rows], v_t[:, rows]
            )
        )
    att_t, gq_t, gk_t, gv_t = (jnp.concatenate(p, axis=1) for p in zip(*parts))
    mixed = dot_nn(flip(att_t), wo)
    mixed_ref[...] = from_groups(mixed, members, cells).astype(BF16)
    grad_in = (dot_nn(wq, gq_t) + dot_nn(wk, gk_t) + dot_nn(wv, gv_t)).T
    grads_ref[0:width] = dot_nt(in_t, gq_t)
    grads_ref[width : 2 * width] = dot_nt(in_t, gk_t)
    grads_ref[2 * width : 3 * width] = dot_nt(in_t, gv_t)
    grads_ref[3 * width : 4 * width] = dot_nn(att_t, gm)
    gain_out_ref[...] = jnp.sum(grad_in * normed, axis=0, keepdims=True)
    grad_normed = grad_in * gain_ref[...]
    corr = inv * (grad_normed - normed * jnp.mean(grad_normed * normed, axis=-1, keepdims=True))
    corr_ref[...] = from_groups(corr, members, cells).astype(BF16)


def block(f, gm, gain, wq, wk, wv, wo, interpret=False):
    width = f.shape[-1]
    return pl.pallas_call(
        block_kernel,
        out_shape=(
            jax.ShapeDtypeStruct(f.shape, BF16),
            jax.ShapeDtypeStruct(f.shape, BF16),
            jax.ShapeDtypeStruct((4 * width, width), F32),
            jax.ShapeDtypeStruct((1, width), F32),
        ),
        interpret=interpret,
        compiler_params=pltpu.CompilerParams(vmem_limit_bytes=48 * 2**20),
    )(f, gm, gain.reshape(1, -1), wq, wk, wv, wo)


def with_halo(x, sides, width):
    for axis, dim in sides:
        size, length = (lax.axis_size(axis), x.shape[dim])
        up = [(i, (i + 1) % size) for i in range(size - 1)]
        down = [(j, i) for i, j in up]
        last = lax.slice_in_dim(x, length - width, length, axis=dim)
        first = lax.slice_in_dim(x, 0, width, axis=dim)
        before = lax.ppermute(last, axis, up)
        after = lax.ppermute(first, axis, down)
        x = jnp.concatenate([before, x, after], axis=dim)
    return x


def local(fields, norm_gain, w_query, w_key, w_value, w_out, mix_kernel, cotangent):
    members, tile_rows, tile_cols, width = fields.shape
    cells = tile_rows * tile_cols
    padded_cot = with_halo(cotangent, (("row", 1), ("col", 2)), 1)
    shifts = [
        padded_cot[:, 2 - i : 2 - i + tile_rows, 2 - j : 2 - j + tile_cols, :].astype(F32)
        for i in range(3)
        for j in range(3)
    ]
    taps = mix_kernel.reshape(9, width)
    summed = jnp.zeros(fields.shape, F32)
    for i in range(9):
        summed = summed + taps[i] * shifts[i]
    flat = (members, cells, width)
    sent = jnp.stack([fields.reshape(flat), summed.astype(BF16).reshape(flat)])
    got = lax.all_to_all(sent, "mem", split_axis=2, concat_axis=1, tiled=True)
    corr, mixed, grads, gain = block(got[0], got[1], norm_gain, w_query, w_key, w_value, w_out)
    back = lax.all_to_all(jnp.stack([corr, mixed]), "mem", split_axis=1, concat_axis=2, tiled=True)
    grad_fields = (cotangent.astype(F32) + back[0].reshape(fields.shape).astype(F32)).astype(BF16)
    mixed = back[1].reshape(fields.shape).astype(F32)
    terms = jnp.stack([jnp.sum(s * mixed, axis=(0, 1, 2)) for s in shifts])
    total = lax.psum(jnp.concatenate([grads, gain, terms]), ("mem", "row", "col"))
    tokens = math.prod(fields.shape[:3]) * math.prod(
        lax.axis_size(a) for a in ("mem", "row", "col")
    )
    total = total * (1.0 / math.sqrt(tokens))
    w = [total[i * width : (i + 1) * width] for i in range(4)]
    return (grad_fields, total[4 * width], *w, total[4 * width + 1 :].reshape(3, 3, width))


def solution(mesh):
    tile = P("mem", "row", "col", None)
    in_specs = (tile, P(), P(), P(), P(), P(), P(), tile)
    out_specs = (tile, P(), P(), P(), P(), P(), P())
    return jax.shard_map(local, mesh=mesh, in_specs=in_specs, out_specs=out_specs, check_vma=False)
```

time: 427 us -> 208 us (0.49)
  matrix products: 149 us -> 0 us
  local copies, waits for them, and re-layouts: 58.4 us -> 9.33 us
  blocking collectives: 67.9 us -> 22.6 us
  waiting for transfers between devices: 112 us -> 136 us
  Pallas kernels: 0 us -> 9.69 us
  other arithmetic: 10.3 us -> 3.9 us
    dot_general x34 -> x0, matrix products: 138 us -> none  [the longest x2 53.6 us: one_block(): jnp.einsum('chmn,mche->nche', grad_score, query_heads, preferred_element_...]
    psum x1 -> x0, blocking collectives: 39.6 us -> none  [local(): lax.psum((acc_q, acc_k, acc_v, acc_out, acc_gain, local_kernel), ('mem',...]
    psum x1, waiting for transfers between devices: 93.5 us -> 129 us  [local(): lax.psum(jnp.concatenate([grads, gain, terms]), ('mem', 'row', 'col'))]
    all_gather x4 -> x0, blocking collectives: 28.3 us -> none  [the longest x2 14.6 us: one_block(): lax.all_gather(value_proj, 'mem', axis=0, tiled=True)]
    convert_element_type x14 -> x1, local copies, waits for them, and re-layouts: 23.1 us -> 0.21 us  [local(): sent = jnp.stack([fields.reshape(flat), summed.astype(BF16).reshape(flat)])]
    all_to_all x0 -> x2, blocking collectives: none -> 22.6 us  [the longest x1 11.4 us: local(): got = lax.all_to_all(sent, 'mem', split_axis=2, concat_axis=1, tiled=True)]
    reshape x13 -> x2, local copies, waits for them, and re-layouts: 21.2 us -> 1.33 us  [the longest x1 0.72 us: local(): taps = mix_kernel.reshape(9, width)]
    reduce_scatter x4 -> x0, waiting for transfers between devices: 13.7 us -> none  [the longest x2 13.7 us: one_block(): lax.psum_scatter(part_v.astype(jnp.bfloat16), 'mem', scatter_dimension=0,...]
  transfers between devices with their start and end apart: 9 -> 5, of which waited for: 6 -> 3; matrix products, arithmetic and copies ran while one was open for 23% -> 1% of each run, Pallas kernels for 0% -> 0%
where the time goes in v1:
time: 208 us; the launch traced here: 207 us
  waiting for transfers between devices  136 us (65%)
  blocking collectives  22.6 us (11%)
  between operations  14.3 us (7%)
  starting transfers between devices  11 us (5%)
  Pallas kernels  9.69 us (5%)
  local copies, waits for them, and re-layouts  9.33 us (4%)
  other arithmetic  3.9 us (2%)
    psum x1, waiting for transfers between devices, local(): lax.psum(jnp.concatenate([grads, gain, terms]), ('mem', 'row', 'col'))  129 us
    all_to_all x1, blocking collectives, local(): got = lax.all_to_all(sent, 'mem', split_axis=2, concat_axis=1, tiled=True)  11.4 us
    all_to_all x1, blocking collectives, local(): lax.all_to_all(jnp.stack([corr, mixed]), 'mem', split_axis=1, concat_axis...  11.2 us
    pallas_call x1, Pallas kernels, block(): pl.pallas_call(block_kernel, out_shape=(jax.ShapeDtypeStruct(f.shape, BF1...  9.69 us
    ppermute x2, starting transfers between devices, with_halo(): before = lax.ppermute(last, axis, up)  8.38 us
    ppermute x2, waiting for transfers between devices, with_halo(): after = lax.ppermute(first, axis, down)  7.32 us
  transfers between devices with their start and end apart: 5, of which 3 were waited for; matrix products, arithmetic and copies ran while one was open for 1% of the time, Pallas kernels for 0%

profile of v1, /device:TPU:0, one launch (start us, length us, event | category | flops | bytes accessed | tf_op | source)
XLA Modules:
  0.0 207.1 jit_solution(18346188985050525473)
XLA Ops:
  7.2 0.0 all-reduce.2.cloned.1.call-start
  7.2 0.9 fusion.26
  8.2 5.0 %collective-permute-start = (bf16[4,1,32,256]{3,2,1,0:T(8,128)(2,1)S(1)}, bf16[4,1,32,256]{3,2,1,0:T(8,128)(2,1)S(1)}, u32[]{:S(2)}, u32[]{:S(2)}) collective-permute-start(bf16[4,1,32,256]{3,2,1,0:T(8,128)(2,1)S(1)} %get-tuple-element.37), channel_id=1, source_target_pairs={{0,2},{2,4},{4,6},{1,3},{3,5},{5,7},{8,10},{10,12},{12,14},{9,11},... | collective-permute-start | bytes 196616 | tf_op jit(solution)/shard_map/ppermute | solution.py:140
  13.2 1.3 collective-permute-start.1
  14.4 0.7 reshape.44
  15.2 1.0 constant_dynamic-update-slice_fusion.1
  16.2 3.2 %collective-permute-done.1 = bf16[4,1,32,256]{3,2,1,0:T(8,128)(2,1)S(1)} collective-permute-done((bf16[4,1,32,256]{3,2,1,0:T(8,128)(2,1)S(1)}, bf16[4,1,32,256]{3,2,1,0:T(8,128)(2,1)S(1)}, u32[]{:S(2)}, u32[]{:S(2)}) %collective-permute-start.1) | collective-permute-done | bytes 65568 | tf_op jit(solution)/shard_map/ppermute | solution.py:141
  19.4 3.4 %collective-permute-start.3 = (bf16[4,6,1,256]{3,2,1,0:T(2,128)(2,1)S(1)}, bf16[4,6,1,256]{3,2,1,0:T(2,128)(2,1)S(1)}, u32[]{:S(2)}, u32[]{:S(2)}) collective-permute-start(bf16[4,6,1,256]{3,2,1,0:T(2,128)(2,1)S(1)} %get-tuple-element.34), channel_id=1, source_target_pairs={{0,1},{2,3},{4,5},{6,7},{8,9},{10,11},{12,13},{14,15},{16,17},{18,... | collective-permute-start | bytes 36872 | tf_op jit(solution)/shard_map/ppermute | solution.py:140
  22.8 1.3 collective-permute-start.2
  24.1 0.2 copy.19
  24.3 4.2 %collective-permute-done.2 = bf16[4,6,1,256]{3,2,1,0:T(2,128)(2,1)S(1)} collective-permute-done((bf16[4,6,1,256]{3,2,1,0:T(2,128)(2,1)S(1)}, bf16[4,6,1,256]{3,2,1,0:T(2,128)(2,1)S(1)}, u32[]{:S(2)}, u32[]{:S(2)}) %collective-permute-start.2) | collective-permute-done | bytes 12320 | tf_op jit(solution)/shard_map/ppermute | solution.py:141
  28.5 0.7 fusion.8
  29.3 0.2 copy.20
  29.5 0.3 pad_maximum_fusion
  29.8 11.4 %all_to_all.30 = bf16[2,4,128,256]{3,1,0,2:T(4,128)(2,1)S(1)} all-to-all(bf16[2,4,128,256]{3,1,0,2:T(4,128)(2,1)S(1)} %pad_maximum_fusion), channel_id=1, replica_groups=mesh['mem'=4,'row'=4,'col'=2] {'mem'}, dimensions={2} | all-to-all | bytes 1048576 | tf_op jit(solution)/shard_map/all_to_all | solution.py:161
  41.2 0.1 copy.21
  41.5 0.7 copy-done
  42.2 0.1 copy-done.1
  42.3 0.1 copy-done.2
  42.4 0.1 copy-done.3
  42.4 9.7 %shard_map.135 = (bf16[16,32,256]{2,1,0:T(8,128)(2,1)S(1)}, bf16[16,32,256]{2,1,0:T(8,128)(2,1)S(1)}, f32[1024,256]{1,0:T(8,128)S(1)}, f32[1,256]{1,0:T(1,128)S(1)}) custom-call(bf16[16,32,256]{2,1,0:T(8,128)(2,1)S(1)} %bitcast.60, bf16[16,32,256]{2,1,0:T(8,128)(2,1)S(1)} %bitcast.59, f32[1,256]{1,0:T(1,128)S(1)} %bitcast.63, bf16[256,256]{1,0:T(8,128)(2,1)S(1)} %copy-done, ...), custom_call_target="tpu_custom_call" | custom-call | tf_op jit(solution)/shard_map/pallas_call | solution.py:120
  52.1 0.1 pad_maximum_fusion.1
  52.2 11.2 %all_to_all.31 = bf16[2,16,32,256]{3,2,0,1:T(8,128)(2,1)S(1)} all-to-all(bf16[2,16,32,256]{3,2,0,1:T(8,128)(2,1)S(1)} %copy.24), channel_id=1, replica_groups=mesh['mem'=4,'row'=4,'col'=2] {'mem'}, dimensions={1} | all-to-all | bytes 1048576 | tf_op jit(solution)/shard_map/all_to_all | solution.py:163
  63.5 0.6 fusion.18
  64.0 0.9 fusion.17
  64.9 2.8 %concatenate.28 = f32[1034,256]{1,0:T(8,128)} concatenate(f32[1024,256]{1,0:T(8,128)S(1)} %get-tuple-element.13, f32[1,256]{1,0:T(1,128)S(1)} %get-tuple-element.14, f32[1,256]{1,0:T(1,128)S(1)} %bitcast.74, f32[1,256]{1,0:T(1,128)S(1)} %bitcast.78, f32[1,256]{1,0:T(1,128)S(1)} %bitcast.71, f32[1,256]{1,0:T(1,128)S(1)} %bitcast.73, f32[1,256]{1,0:T(1,128)S(1)} %bitcast.77, ...), dimensions={0} | concatenate | bytes 2117632 | tf_op jit(solution)/shard_map/concatenate | solution.py:167
  67.8 0.0 all-reduce.2.cloned.1.call-update
  67.8 129.0 %all-reduce.2.cloned.1.call-done = f32[1034,256]{1,0:T(8,128)} async-done(((f32[1034,256]{1,0:T(8,128)}), f32[1034,256]{1,0:T(8,128)}) %all-reduce.2.cloned.1.call-update) | async-done | bytes 1058832 | tf_op jit(solution)/shard_map/psum | solution.py:167
  196.8 1.3 broadcast_multiply_fusion
  198.1 0.6 slice.159
  198.7 1.0 fusion.23
  199.7 0.6 reshape.46
  (22 shorter events, 0.3 us)
Async XLA Ops:
  7.2 21.4 %copy-start.5 = (bf16[4,4,32,256]{3,2,1,0:T(8,128)(2,1)S(1)}, bf16[4,4,32,256]{3,2,1,0:T(8,128)(2,1)}, u32[]{:S(2)}) copy-start(bf16[4,4,32,256]{3,2,1,0:T(8,128)(2,1)} %param.15) | copy-start | bytes 786436
  7.2 16.9 %copy-start.6 = (bf16[4,4,32,256]{3,2,1,0:T(8,128)(2,1)S(1)}, bf16[4,4,32,256]{3,2,1,0:T(8,128)(2,1)}, u32[]{:S(2)}) copy-start(bf16[4,4,32,256]{3,2,1,0:T(8,128)(2,1)} %param.8) | copy-start | bytes 786436
  7.2 189.6 %all-reduce.2.cloned.1.call-start = ((), (), s32[]{:S(2)}) async-start(), calls=%async_computation.2 | async-start | bytes 2129920 | tf_op jit(solution)/shard_map/psum | solution.py:167
  8.2 7.0 %collective-permute-start = (bf16[4,1,32,256]{3,2,1,0:T(8,128)(2,1)S(1)}, bf16[4,1,32,256]{3,2,1,0:T(8,128)(2,1)S(1)}, u32[]{:S(2)}, u32[]{:S(2)}) collective-permute-start(bf16[4,1,32,256]{3,2,1,0:T(8,128)(2,1)S(1)} %get-tuple-element.37), channel_id=1, source_target_pairs={{0,2},{2,4},{4,6},{1,3},{3,5},{5,7},{8,10},{10,12},{12,14},{9,11},... | collective-permute-start | bytes 196616 | tf_op jit(solution)/shard_map/ppermute | solution.py:140
  13.2 6.2 %collective-permute-start.1 = (bf16[4,1,32,256]{3,2,1,0:T(8,128)(2,1)S(1)}, bf16[4,1,32,256]{3,2,1,0:T(8,128)(2,1)S(1)}, u32[]{:S(2)}, u32[]{:S(2)}) collective-permute-start(bf16[4,1,32,256]{3,2,1,0:T(8,128)(2,1)S(1)} %get-tuple-element.36), channel_id=1, source_target_pairs={{2,0},{4,2},{6,4},{3,1},{5,3},{7,5},{10,8},{12,10},{14,12},{11,9},... | collective-permute-start | bytes 196616 | tf_op jit(solution)/shard_map/ppermute | solution.py:141
  19.4 5.0 %collective-permute-start.3 = (bf16[4,6,1,256]{3,2,1,0:T(2,128)(2,1)S(1)}, bf16[4,6,1,256]{3,2,1,0:T(2,128)(2,1)S(1)}, u32[]{:S(2)}, u32[]{:S(2)}) collective-permute-start(bf16[4,6,1,256]{3,2,1,0:T(2,128)(2,1)S(1)} %get-tuple-element.34), channel_id=1, source_target_pairs={{0,1},{2,3},{4,5},{6,7},{8,9},{10,11},{12,13},{14,15},{16,17},{18,... | collective-permute-start | bytes 36872 | tf_op jit(solution)/shard_map/ppermute | solution.py:140
  22.8 5.7 %collective-permute-start.2 = (bf16[4,6,1,256]{3,2,1,0:T(2,128)(2,1)S(1)}, bf16[4,6,1,256]{3,2,1,0:T(2,128)(2,1)S(1)}, u32[]{:S(2)}, u32[]{:S(2)}) collective-permute-start(bf16[4,6,1,256]{3,2,1,0:T(2,128)(2,1)S(1)} %get-tuple-element.35), channel_id=1, source_target_pairs={{1,0},{3,2},{5,4},{7,6},{9,8},{11,10},{13,12},{15,14},{17,16},{19,... | collective-permute-start | bytes 36872 | tf_op jit(solution)/shard_map/ppermute | solution.py:141
  41.3 0.9 copy-start
  41.3 1.0 copy-start.1
  41.3 1.0 copy-start.2
  41.3 1.1 copy-start.3
  41.4 1.1 copy-start.4
Sparse Core Ops, SparseCore 0:
  67.9 128.8 all-reduce.1

commit v2 on v1

--- a/solution.py
+++ b/solution.py
@@ -130,6 +130,211 @@
     )(f, gm, gain.reshape(1, -1), wq, wk, wv, wo)
 
 
+MESH = pl.DeviceIdType.MESH
+VMEM_SPEC = pl.BlockSpec(memory_space=pltpu.VMEM)
+
+
+def enter(peers):
+    barrier = pltpu.get_barrier_semaphore()
+    for peer in peers:
+        pl.semaphore_signal(barrier, inc=1, device_id=peer, device_id_type=MESH)
+    pl.semaphore_wait(barrier, len(peers))
+
+
+def push(src, dst, send_sem, recv_sem, peer):
+    return pltpu.make_async_remote_copy(
+        src_ref=src, dst_ref=dst, send_sem=send_sem, recv_sem=recv_sem,
+        device_id=peer, device_id_type=MESH,
+    )
+
+
+def exchange_kernel(count, inward, *refs):
+    srcs, dsts, (send, recv) = refs[:2], refs[2:4], refs[4:]
+    me = lax.axis_index("mem")
+    row, col = lax.axis_index("row"), lax.axis_index("col")
+    others = [lax.rem(me + k, count) for k in range(1, count)]
+    enter([(o, row, col) for o in others])
+
+    def view(ref, i, by_chunk):
+        return ref.at[:, i] if by_chunk else ref.at[i]
+
+    copies = []
+    for t in range(2):
+        for o in others:
+            copy = push(
+                view(srcs[t], o, inward), view(dsts[t], me, not inward),
+                send.at[t, o], recv.at[t, me], (o, row, col),
+            )
+            copy.start()
+            copies.append(copy)
+    for t in range(2):
+        if inward:
+            dsts[t][me] = srcs[t][:, me]
+        else:
+            dsts[t][:, me] = srcs[t][me]
+    for copy in copies:
+        copy.wait_send()
+    for t in range(2):
+        for o in others:
+            push(
+                view(srcs[t], o, inward), view(dsts[t], o, not inward),
+                send.at[t, o], recv.at[t, o], (o, row, col),
+            ).wait_recv()
+
+
+def exchange(a, b, inward, collective_id):
+    count = lax.axis_size("mem")
+    shape = a.shape
+    out = (shape[1], shape[0]) + shape[2:]
+    return pl.pallas_call(
+        functools.partial(exchange_kernel, count, inward),
+        out_shape=(jax.ShapeDtypeStruct(out, a.dtype),) * 2,
+        in_specs=[VMEM_SPEC] * 2,
+        out_specs=(VMEM_SPEC,) * 2,
+        scratch_shapes=[pltpu.SemaphoreType.DMA((2, count))] * 2,
+        compiler_params=pltpu.CompilerParams(collective_id=collective_id, has_side_effects=True),
+    )(a, b)
+
+
+def sum_kernel(
+    planes, rows, cols, scale,
+    g_ref, s_ref, out_ref, sout_ref,
+    a_src, a_dst, acc1, b_src, b_dst, acc2, c_src, c_dst, gz, gp, ga, s_a, s_b, s_c,
+    send_a, recv_a, send_b, recv_b, send_c, recv_c,
+    send_z, recv_z, send_p, recv_p, send_g, recv_g,
+    ssend_b, srecv_b, ssend_c, srecv_c, ssend_a, srecv_a,
+):
+    mem, row, col = (lax.axis_index(a) for a in ("mem", "row", "col"))
+    core = lax.rem(mem, 2)
+    other = 1 - core
+    me_p = lax.div(mem, 2) * cols + col
+    partner = (mem + 1 - 2 * core, row, col)
+
+    def plane_peer(p):
+        return (lax.div(p, cols) * 2 + core, row, lax.rem(p, cols))
+
+    plane_others = [lax.rem(me_p + k, planes) for k in range(1, planes)]
+    row_others = [lax.rem(row + k, rows) for k in range(1, rows)]
+    enter(
+        [partner]
+        + [plane_peer(p) for p in plane_others]
+        + [(mem, r, col) for r in row_others]
+    )
+
+    a_src[...] = g_ref[other].astype(BF16)
+    first = push(a_src, a_dst, send_a, recv_a, partner)
+    first.start()
+    s_a[core] = s_ref[...]
+    small = push(s_a.at[core], s_a.at[core], ssend_a, srecv_a, partner)
+    small.start()
+    first.wait()
+    acc1[...] = g_ref[core] + a_dst[...].astype(F32)
+    b_src[...] = acc1[...].astype(BF16)
+
+    sent = []
+    for p in plane_others:
+        copy = push(b_src.at[p], b_dst.at[me_p], send_b.at[p], recv_b.at[me_p], plane_peer(p))
+        copy.start()
+        sent.append(copy)
+    small.wait_send()
+    push(s_a.at[other], s_a.at[other], ssend_a, srecv_a, partner).wait_recv()
+    s_b[me_p] = s_a[0] + s_a[1]
+    for p in plane_others:
+        copy = push(s_b.at[me_p], s_b.at[me_p], ssend_b.at[p], srecv_b.at[me_p], plane_peer(p))
+        copy.start()
+        sent.append(copy)
+    acc2[...] = acc1[me_p]
+    for p in plane_others:
+        push(b_src.at[p], b_dst.at[p], send_b.at[p], recv_b.at[p], plane_peer(p)).wait_recv()
+        acc2[...] += b_dst[p].astype(F32)
+    c_src[...] = acc2[...].astype(BF16)
+
+    for r in row_others:
+        copy = push(c_src.at[r], c_dst.at[row], send_c.at[r], recv_c.at[row], (mem, r, col))
+        copy.start()
+        sent.append(copy)
+    for p in plane_others:
+        push(s_b.at[p], s_b.at[p], ssend_b.at[p], srecv_b.at[p], plane_peer(p)).wait_recv()
+    total = s_b[0]
+    for p in range(1, planes):
+        total = total + s_b[p]
+    s_c[row] = total
+    for r in row_others:
+        copy = push(s_c.at[row], s_c.at[row], ssend_c.at[r], srecv_c.at[row], (mem, r, col))
+        copy.start()
+        sent.append(copy)
+    whole = acc2[row]
+    for r in row_others:
+        push(c_src.at[r], c_dst.at[r], send_c.at[r], recv_c.at[r], (mem, r, col)).wait_recv()
+        whole = whole + c_dst[r].astype(F32)
+    gz[row] = (whole * scale).astype(BF16)
+
+    for r in row_others:
+        copy = push(gz.at[row], gz.at[row], send_z.at[r], recv_z.at[row], (mem, r, col))
+        copy.start()
+        sent.append(copy)
+    for r in row_others:
+        push(s_c.at[r], s_c.at[r], ssend_c.at[r], srecv_c.at[r], (mem, r, col)).wait_recv()
+    total = s_c[0]
+    for r in range(1, rows):
+        total = total + s_c[r]
+    sout_ref[...] = total * scale
+    for r in row_others:
+        push(gz.at[r], gz.at[r], send_z.at[r], recv_z.at[r], (mem, r, col)).wait_recv()
+    for p in plane_others:
+        copy = push(gz, gp.at[me_p], send_p.at[p], recv_p.at[me_p], plane_peer(p))
+        copy.start()
+        sent.append(copy)
+    own = push(gz, ga.at[me_p], send_g.at[me_p], recv_g.at[me_p], partner)
+    own.start()
+    sent.append(own)
+    out_ref[core, me_p] = gz[...].astype(F32)
+    for p in plane_others:
+        push(gz, gp.at[p], send_p.at[p], recv_p.at[p], plane_peer(p)).wait_recv()
+        copy = push(gp.at[p], ga.at[p], send_g.at[p], recv_g.at[p], partner)
+        copy.start()
+        sent.append(copy)
+        out_ref[core, p] = gp[p].astype(F32)
+    for p in [me_p] + plane_others:
+        push(gz, ga.at[p], send_g.at[p], recv_g.at[p], partner).wait_recv()
+        out_ref[other, p] = ga[p].astype(F32)
+    for copy in sent:
+        copy.wait_send()
+
+
+def sum_all(grads, small, scale, collective_id):
+    rows, cols = lax.axis_size("row"), lax.axis_size("col")
+    planes = lax.axis_size("mem") // 2 * cols
+    height, width = grads.shape
+    unit = (height // (2 * planes * rows), width)
+    part, half = (rows,) + unit, (planes, rows) + unit
+    full = (2,) + half
+    sems = pltpu.SemaphoreType.DMA
+    out, sout = pl.pallas_call(
+        functools.partial(sum_kernel, planes, rows, cols, scale),
+        out_shape=(jax.ShapeDtypeStruct(full, F32), jax.ShapeDtypeStruct(small.shape, F32)),
+        in_specs=[VMEM_SPEC] * 2,
+        out_specs=(VMEM_SPEC,) * 2,
+        scratch_shapes=[
+            pltpu.VMEM(half, BF16), pltpu.VMEM(half, BF16), pltpu.VMEM(half, F32),
+            pltpu.VMEM(half, BF16), pltpu.VMEM(half, BF16), pltpu.VMEM(part, F32),
+            pltpu.VMEM(part, BF16), pltpu.VMEM(part, BF16), pltpu.VMEM(part, BF16),
+            pltpu.VMEM(half, BF16), pltpu.VMEM(half, BF16),
+            pltpu.VMEM((2,) + small.shape, F32),
+            pltpu.VMEM((planes,) + small.shape, F32),
+            pltpu.VMEM((rows,) + small.shape, F32),
+            sems(()), sems(()), sems((planes,)), sems((planes,)), sems((rows,)), sems((rows,)),
+            sems((rows,)), sems((rows,)), sems((planes,)), sems((planes,)),
+            sems((planes,)), sems((planes,)),
+            sems((planes,)), sems((planes,)), sems((rows,)), sems((rows,)), sems(()), sems(()),
+        ],
+        compiler_params=pltpu.CompilerParams(
+            collective_id=collective_id, has_side_effects=True, vmem_limit_bytes=48 * 2**20
+        ),
+    )(grads.reshape(full), small)
+    return out.reshape(height, width), sout
+
+
 def with_halo(x, sides, width):
     for axis, dim in sides:
         size, length = (lax.axis_size(axis), x.shape[dim])
@@ -156,21 +361,25 @@
     summed = jnp.zeros(fields.shape, F32)
     for i in range(9):
         summed = summed + taps[i] * shifts[i]
-    flat = (members, cells, width)
-    sent = jnp.stack([fields.reshape(flat), summed.astype(BF16).reshape(flat)])
-    got = lax.all_to_all(sent, "mem", split_axis=2, concat_axis=1, tiled=True)
-    corr, mixed, grads, gain = block(got[0], got[1], norm_gain, w_query, w_key, w_value, w_out)
-    back = lax.all_to_all(jnp.stack([corr, mixed]), "mem", split_axis=1, concat_axis=2, tiled=True)
-    grad_fields = (cotangent.astype(F32) + back[0].reshape(fields.shape).astype(F32)).astype(BF16)
-    mixed = back[1].reshape(fields.shape).astype(F32)
-    terms = jnp.stack([jnp.sum(s * mixed, axis=(0, 1, 2)) for s in shifts])
-    total = lax.psum(jnp.concatenate([grads, gain, terms]), ("mem", "row", "col"))
+    count = lax.axis_size("mem")
+    split = (members, count, cells // count, width)
+    f_got, gm_got = exchange(fields.reshape(split), summed.astype(BF16).reshape(split), True, 1)
+    joined = (members * count, cells // count, width)
+    corr, mixed, grads, gain = block(
+        f_got.reshape(joined), gm_got.reshape(joined), norm_gain, w_query, w_key, w_value, w_out
+    )
+    sender = (count, members, cells // count, width)
+    corr, mixed = exchange(corr.reshape(sender), mixed.reshape(sender), False, 2)
+    grad_fields = (cotangent.astype(F32) + corr.reshape(fields.shape).astype(F32)).astype(BF16)
+    mixed = mixed.reshape(fields.shape).astype(F32)
+    terms = [jnp.sum(s * mixed, axis=(0, 1, 2))[None] for s in shifts]
+    small = jnp.concatenate([gain, *terms, jnp.zeros((6, width), F32)])
     tokens = math.prod(fields.shape[:3]) * math.prod(
         lax.axis_size(a) for a in ("mem", "row", "col")
     )
-    total = total * (1.0 / math.sqrt(tokens))
+    total, small = sum_all(grads, small, 1.0 / math.sqrt(tokens), 3)
     w = [total[i * width : (i + 1) * width] for i in range(4)]
-    return (grad_fields, total[4 * width], *w, total[4 * width + 1 :].reshape(3, 3, width))
+    return (grad_fields, small[0], *w, small[1:10].reshape(3, 3, width))
 
 
 def solution(mesh):

time: 208 us -> 84.5 us (0.41)
  waiting for transfers between devices: 136 us -> 5.57 us
  Pallas kernels: 9.69 us -> 53.8 us
  blocking collectives: 22.6 us -> 0 us
  between operations: 14.3 us -> 0.82 us
    psum x1 -> x0, waiting for transfers between devices: 129 us -> none  [local(): lax.psum(jnp.concatenate([grads, gain, terms]), ('mem', 'row', 'col'))]
    pallas_call x0 -> x3, Pallas kernels: none -> 44.2 us  [the longest x1 24.3 us: sum_all(): pl.pallas_call(functools.partial(sum_kernel, planes, rows, cols, scale),...]
    all_to_all x2 -> x0, blocking collectives: 22.6 us -> none  [the longest x1 11.4 us: local(): got = lax.all_to_all(sent, 'mem', split_axis=2, concat_axis=1, tiled=True)]
    ppermute x2, waiting for transfers between devices: 7.32 us -> 4.09 us  [with_halo(): after = lax.ppermute(first, axis, down)]
    concatenate x1, local copies, waits for them, and re-layouts: 2.83 us -> 0.05 us  [local(): small = jnp.concatenate([gain, *terms, jnp.zeros((6, width), F32)])]
  transfers between devices with their start and end apart: 5 -> 4, of which waited for: 3 -> 2; matrix products, arithmetic and copies ran while one was open for 1% -> 1% of each run, Pallas kernels for 0% -> 0%
where the time goes in v2:
time: 84.5 us; the launch traced here: 84.1 us
  Pallas kernels  53.8 us (64%)
  starting transfers between devices  12.1 us (14%)
  local copies, waits for them, and re-layouts  7.89 us (9%)
  waiting for transfers between devices  5.57 us (7%)
  other arithmetic  3.92 us (5%)
    pallas_call x1, Pallas kernels, sum_all(): pl.pallas_call(functools.partial(sum_kernel, planes, rows, cols, scale),...  24.3 us
    pallas_call x2, Pallas kernels, exchange(): pl.pallas_call(functools.partial(exchange_kernel, count, inward), out_sha...  19.8 us
    pallas_call x1, Pallas kernels, block(): pl.pallas_call(block_kernel, out_shape=(jax.ShapeDtypeStruct(f.shape, BF1...  9.68 us
    ppermute x2, starting transfers between devices, with_halo(): before = lax.ppermute(last, axis, up)  9.5 us
    ppermute x2, waiting for transfers between devices, with_halo(): after = lax.ppermute(first, axis, down)  4.09 us
    unnamed x22, local copies, waits for them, and re-layouts  3.98 us
    ppermute x2, starting transfers between devices, with_halo(): after = lax.ppermute(first, axis, down)  2.58 us
    reduce_sum x1, other arithmetic, local(): terms = [jnp.sum(s * mixed, axis=(0, 1, 2))[None] for s in shifts]  2.49 us
  transfers between devices with their start and end apart: 4, of which 2 were waited for; matrix products, arithmetic and copies ran while one was open for 1% of the time, Pallas kernels for 0%

profile of v2, /device:TPU:0, one launch (start us, length us, event | category | flops | bytes accessed | tf_op | source)
XLA Modules:
  0.0 84.1 jit_solution(4994894142099890883)
XLA Ops:
  0.6 0.0 copy-start.9
  0.6 0.9 %fusion.25 = (bf16[4,1,32,256]{3,2,1,0:T(8,128)(2,1)S(1)}, bf16[4,1,32,256]{3,2,1,0:T(8,128)(2,1)S(1)}) fusion(bf16[4,4,32,256]{3,2,1,0:T(8,128)(2,1)} %param.15), kind=kLoop, calls=%fused_computation.59 | loop fusion | bytes 262144 | tf_op jit(solution)/shard_map/slice | solution.py:344
  1.6 5.0 %collective-permute-start = (bf16[4,1,32,256]{3,2,1,0:T(8,128)(2,1)S(1)}, bf16[4,1,32,256]{3,2,1,0:T(8,128)(2,1)S(1)}, u32[]{:S(2)}, u32[]{:S(2)}) collective-permute-start(bf16[4,1,32,256]{3,2,1,0:T(8,128)(2,1)S(1)} %get-tuple-element.50), channel_id=1, source_target_pairs={{0,2},{2,4},{4,6},{1,3},{3,5},{5,7},{8,10},{10,12},{12,14},{9,11},... | collective-permute-start | bytes 196616 | tf_op jit(solution)/shard_map/ppermute | solution.py:345
  6.5 1.3 %collective-permute-start.1 = (bf16[4,1,32,256]{3,2,1,0:T(8,128)(2,1)S(1)}, bf16[4,1,32,256]{3,2,1,0:T(8,128)(2,1)S(1)}, u32[]{:S(2)}, u32[]{:S(2)}) collective-permute-start(bf16[4,1,32,256]{3,2,1,0:T(8,128)(2,1)S(1)} %get-tuple-element.49), channel_id=1, source_target_pairs={{2,0},{4,2},{6,4},{3,1},{5,3},{7,5},{10,8},{12,10},{14,12},{11,9},... | collective-permute-start | bytes 196616 | tf_op jit(solution)/shard_map/ppermute | solution.py:346
  7.8 0.7 reshape.50
  8.6 0.0 collective-permute-done
  8.6 0.0 copy-done.9
  8.6 4.1 %collective-permute-done.1 = bf16[4,1,32,256]{3,2,1,0:T(8,128)(2,1)S(1)} collective-permute-done((bf16[4,1,32,256]{3,2,1,0:T(8,128)(2,1)S(1)}, bf16[4,1,32,256]{3,2,1,0:T(8,128)(2,1)S(1)}, u32[]{:S(2)}, u32[]{:S(2)}) %collective-permute-start.1) | collective-permute-done | bytes 65568 | tf_op jit(solution)/shard_map/ppermute | solution.py:346
  12.8 1.3 %collective-permute-start.2 = (bf16[4,6,1,256]{3,2,1,0:T(2,128)(2,1)S(1)}, bf16[4,6,1,256]{3,2,1,0:T(2,128)(2,1)S(1)}, u32[]{:S(2)}, u32[]{:S(2)}) collective-permute-start(bf16[4,6,1,256]{3,2,1,0:T(2,128)(2,1)S(1)} %get-tuple-element.47), channel_id=1, source_target_pairs={{1,0},{3,2},{5,4},{7,6},{9,8},{11,10},{13,12},{15,14},{17,16},{19,... | collective-permute-start | bytes 36872 | tf_op jit(solution)/shard_map/ppermute | solution.py:346
  14.1 4.5 %collective-permute-start.3 = (bf16[4,6,1,256]{3,2,1,0:T(2,128)(2,1)S(1)}, bf16[4,6,1,256]{3,2,1,0:T(2,128)(2,1)S(1)}, u32[]{:S(2)}, u32[]{:S(2)}) collective-permute-start(bf16[4,6,1,256]{3,2,1,0:T(2,128)(2,1)S(1)} %get-tuple-element.46), channel_id=1, source_target_pairs={{0,1},{2,3},{4,5},{6,7},{8,9},{10,11},{12,13},{14,15},{16,17},{18,... | collective-permute-start | bytes 36872 | tf_op jit(solution)/shard_map/ppermute | solution.py:345
  18.6 0.0 collective-permute-done.2
  18.6 1.5 %collective-permute-done.3 = bf16[4,6,1,256]{3,2,1,0:T(2,128)(2,1)S(1)} collective-permute-done((bf16[4,6,1,256]{3,2,1,0:T(2,128)(2,1)S(1)}, bf16[4,6,1,256]{3,2,1,0:T(2,128)(2,1)S(1)}, u32[]{:S(2)}, u32[]{:S(2)}) %collective-permute-start.3) | collective-permute-done | bytes 12320 | tf_op jit(solution)/shard_map/ppermute | solution.py:345
  20.1 1.4 %fusion.8.refs_1_ = bf16[4,4,32,256]{3,2,1,0:T(8,128)(2,1)} fusion(bf16[4,4,32,256]{3,2,1,0:T(8,128)(2,1)S(1)} %copy-done.9, bf16[4,1,32,256]{3,2,1,0:T(8,128)(2,1)S(1)} %collective-permute-done, bf16[4,1,32,256]{3,2,1,0:T(8,128)(2,1)S(1)} %collective-permute-done.1, f32[256]{0:T(256)S(1)} %bitcast.34, f32[256]{0:T(256)S(1)} %bitcast.35, ...), kind=kLoop, calls=%fused_computation.31 | loop fusion | flops 6684672 | bytes 1082368 | tf_op jit(solution)/shard_map/convert_element_type | solution.py:366
  21.5 9.8 %shard_map.135 = (bf16[4,4,32,256]{3,2,1,0:T(8,128)(2,1)}, bf16[4,4,32,256]{3,2,1,0:T(8,128)(2,1)}) custom-call(bf16[4,4,32,256]{3,2,1,0:T(8,128)(2,1)} %refs_0_.1, bf16[4,4,32,256]{3,2,1,0:T(8,128)(2,1)} %fusion.8.refs_1_), custom_call_target="tpu_custom_call" | custom-call | tf_op jit(solution)/shard_map/pallas_call | solution.py:189
  31.4 0.0 copy-start.8
  31.4 0.0 copy-done.4
  31.4 0.0 copy-done.5
  31.4 0.0 copy-done.6
  31.4 0.0 copy-done.7
  31.4 0.6 copy-done.8
  32.0 0.9 %copy-done = bf16[4,4,32,256]{3,2,1,0:T(8,128)(2,1)S(1)} copy-done((bf16[4,4,32,256]{3,2,1,0:T(8,128)(2,1)S(1)}, bf16[4,4,32,256]{3,2,1,0:T(8,128)(2,1)}, u32[]{:S(2)}) %copy-start) | copy-done | bytes 262168
  33.0 0.9 %copy-done.1 = bf16[4,4,32,256]{3,2,1,0:T(8,128)(2,1)S(1)} copy-done((bf16[4,4,32,256]{3,2,1,0:T(8,128)(2,1)S(1)}, bf16[4,4,32,256]{3,2,1,0:T(8,128)(2,1)}, u32[]{:S(2)}) %copy-start.1) | copy-done | bytes 262168
  33.9 9.7 %shard_map.136 = (bf16[16,32,256]{2,1,0:T(8,128)(2,1)S(1)}, bf16[16,32,256]{2,1,0:T(8,128)(2,1)S(1)}, f32[1024,256]{1,0:T(8,128)S(1)}, f32[1,256]{1,0:T(1,128)S(1)}) custom-call(bf16[16,32,256]{2,1,0:T(8,128)(2,1)S(1)} %bitcast.28, bf16[16,32,256]{2,1,0:T(8,128)(2,1)S(1)} %bitcast.29, f32[1,256]{1,0:T(1,128)S(1)} %bitcast.32, ...), custom_call_target="tpu_custom_call" | custom-call | tf_op jit(solution)/shard_map/pallas_call | solution.py:120
  43.6 0.0 copy-start.2
  43.7 0.7 copy-done.2
  44.3 0.7 copy-done.3
  45.0 10.0 %shard_map.137 = (bf16[4,4,32,256]{3,2,1,0:T(8,128)(2,1)}, bf16[4,4,32,256]{3,2,1,0:T(8,128)(2,1)}) custom-call(bf16[4,4,32,256]{3,2,1,0:T(8,128)(2,1)} %bitcast.30, bf16[4,4,32,256]{3,2,1,0:T(8,128)(2,1)} %bitcast.31), custom_call_target="tpu_custom_call" | custom-call | tf_op jit(solution)/shard_map/pallas_call | solution.py:189
  55.1 2.5 %fusion.18 = (f32[256]{0:T(256)S(1)}, f32[256]{0:T(256)S(1)}, f32[256]{0:T(256)S(1)}, f32[256]{0:T(256)S(1)}, f32[256]{0:T(256)S(1)}, /*index=5*/f32[256]{0:T(25...) fusion(bf16[4,4,32,256]{3,2,1,0:T(8,128)(2,1)} %get-tuple-element.24, ...), kind=kLoop, calls=%fused_computation.41 | loop fusion | flops 7206656 | bytes 1606656 | tf_op jit(solution)/shard_map/reduce_sum | solution.py:375
  57.6 24.3 %shard_map.138 = (f32[2,4,4,32,256]{4,3,2,1,0:T(8,128)S(1)}, f32[16,256]{1,0:T(8,128)S(1)}) custom-call(f32[2,4,4,32,256]{4,3,2,1,0:T(8,128)S(1)} %bitcast.26, f32[16,256]{1,0:T(8,128)S(1)} %concatenate.28.s_ref), custom_call_target="tpu_custom_call" | custom-call | tf_op jit(solution)/shard_map/pallas_call | solution.py:313
  82.0 0.6 slice.110
  82.5 1.0 %fusion.23 = (f32[256,256]{1,0:T(8,128)}, f32[256,256]{1,0:T(8,128)}, f32[256,256]{1,0:T(8,128)}, f32[256,256]{1,0:T(8,128)}) fusion(f32[1024,256]{1,0:T(8,128)S(1)} %bitcast.27), kind=kLoop, calls=%fused_computation.57 | loop fusion | bytes 2097152 | tf_op jit(solution)/shard_map/slice | solution.py:381
  83.5 0.6 reshape.58
  (15 shorter events, 0.1 us)
Async XLA Ops:
  0.6 7.9 %copy-start.9 = (bf16[4,4,32,256]{3,2,1,0:T(8,128)(2,1)S(1)}, bf16[4,4,32,256]{3,2,1,0:T(8,128)(2,1)}, u32[]{:S(2)}) copy-start(bf16[4,4,32,256]{3,2,1,0:T(8,128)(2,1)} %param.15) | copy-start | bytes 786436
  1.6 7.0 %collective-permute-start = (bf16[4,1,32,256]{3,2,1,0:T(8,128)(2,1)S(1)}, bf16[4,1,32,256]{3,2,1,0:T(8,128)(2,1)S(1)}, u32[]{:S(2)}, u32[]{:S(2)}) collective-permute-start(bf16[4,1,32,256]{3,2,1,0:T(8,128)(2,1)S(1)} %get-tuple-element.50), channel_id=1, source_target_pairs={{0,2},{2,4},{4,6},{1,3},{3,5},{5,7},{8,10},{10,12},{12,14},{9,11},... | collective-permute-start | bytes 196616 | tf_op jit(solution)/shard_map/ppermute | solution.py:345
  6.5 6.2 %collective-permute-start.1 = (bf16[4,1,32,256]{3,2,1,0:T(8,128)(2,1)S(1)}, bf16[4,1,32,256]{3,2,1,0:T(8,128)(2,1)S(1)}, u32[]{:S(2)}, u32[]{:S(2)}) collective-permute-start(bf16[4,1,32,256]{3,2,1,0:T(8,128)(2,1)S(1)} %get-tuple-element.49), channel_id=1, source_target_pairs={{2,0},{4,2},{6,4},{3,1},{5,3},{7,5},{10,8},{12,10},{14,12},{11,9},... | collective-permute-start | bytes 196616 | tf_op jit(solution)/shard_map/ppermute | solution.py:346
  12.8 5.9 %collective-permute-start.2 = (bf16[4,6,1,256]{3,2,1,0:T(2,128)(2,1)S(1)}, bf16[4,6,1,256]{3,2,1,0:T(2,128)(2,1)S(1)}, u32[]{:S(2)}, u32[]{:S(2)}) collective-permute-start(bf16[4,6,1,256]{3,2,1,0:T(2,128)(2,1)S(1)} %get-tuple-element.47), channel_id=1, source_target_pairs={{1,0},{3,2},{5,4},{7,6},{9,8},{11,10},{13,12},{15,14},{17,16},{19,... | collective-permute-start | bytes 36872 | tf_op jit(solution)/shard_map/ppermute | solution.py:346
  14.1 6.1 %collective-permute-start.3 = (bf16[4,6,1,256]{3,2,1,0:T(2,128)(2,1)S(1)}, bf16[4,6,1,256]{3,2,1,0:T(2,128)(2,1)S(1)}, u32[]{:S(2)}, u32[]{:S(2)}) collective-permute-start(bf16[4,6,1,256]{3,2,1,0:T(2,128)(2,1)S(1)} %get-tuple-element.46), channel_id=1, source_target_pairs={{0,1},{2,3},{4,5},{6,7},{8,9},{10,11},{12,13},{14,15},{16,17},{18,... | collective-permute-start | bytes 36872 | tf_op jit(solution)/shard_map/ppermute | solution.py:345
  21.5 9.8 %copy-start.4 = (bf16[256,256]{1,0:T(8,128)(2,1)S(1)}, bf16[256,256]{1,0:T(8,128)(2,1)}, u32[]{:S(2)}) copy-start(bf16[256,256]{1,0:T(8,128)(2,1)} %wq_ref.1) | copy-start | bytes 393220
  21.5 9.9 %copy-start.5 = (bf16[256,256]{1,0:T(8,128)(2,1)S(1)}, bf16[256,256]{1,0:T(8,128)(2,1)}, u32[]{:S(2)}) copy-start(bf16[256,256]{1,0:T(8,128)(2,1)} %wk_ref.1) | copy-start | bytes 393220
  21.5 9.9 %copy-start.6 = (bf16[256,256]{1,0:T(8,128)(2,1)S(1)}, bf16[256,256]{1,0:T(8,128)(2,1)}, u32[]{:S(2)}) copy-start(bf16[256,256]{1,0:T(8,128)(2,1)} %wv_ref.1) | copy-start | bytes 393220
  21.5 9.9 %copy-start.7 = (bf16[256,256]{1,0:T(8,128)(2,1)S(1)}, bf16[256,256]{1,0:T(8,128)(2,1)}, u32[]{:S(2)}) copy-start(bf16[256,256]{1,0:T(8,128)(2,1)} %wo_ref.1) | copy-start | bytes 393220
  31.4 0.7 copy-start.8
  32.0 0.9 %copy-start = (bf16[4,4,32,256]{3,2,1,0:T(8,128)(2,1)S(1)}, bf16[4,4,32,256]{3,2,1,0:T(8,128)(2,1)}, u32[]{:S(2)}) copy-start(bf16[4,4,32,256]{3,2,1,0:T(8,128)(2,1)} %get-tuple-element.17) | copy-start | bytes 786436
  33.0 0.9 %copy-start.1 = (bf16[4,4,32,256]{3,2,1,0:T(8,128)(2,1)S(1)}, bf16[4,4,32,256]{3,2,1,0:T(8,128)(2,1)}, u32[]{:S(2)}) copy-start(bf16[4,4,32,256]{3,2,1,0:T(8,128)(2,1)} %get-tuple-element.18) | copy-start | bytes 786436
  43.6 0.7 copy-start.2
  44.3 0.7 copy-start.3

commit v3 on v2

--- a/solution.py
+++ b/solution.py
@@ -148,7 +148,8 @@
     )
 
 
-def exchange_kernel(count, inward, *refs):
+def exchange_kernel(count, *refs):
+    inward = False
     srcs, dsts, (send, recv) = refs[:2], refs[2:4], refs[4:]
     me = lax.axis_index("mem")
     row, col = lax.axis_index("row"), lax.axis_index("col")
@@ -182,12 +183,12 @@
             ).wait_recv()
 
 
-def exchange(a, b, inward, collective_id):
+def exchange(a, b, collective_id):
     count = lax.axis_size("mem")
     shape = a.shape
     out = (shape[1], shape[0]) + shape[2:]
     return pl.pallas_call(
-        functools.partial(exchange_kernel, count, inward),
+        functools.partial(exchange_kernel, count),
         out_shape=(jax.ShapeDtypeStruct(out, a.dtype),) * 2,
         in_specs=[VMEM_SPEC] * 2,
         out_specs=(VMEM_SPEC,) * 2,
@@ -334,42 +335,169 @@
     )(grads.reshape(full), small)
     return out.reshape(height, width), sout
 
-
-def with_halo(x, sides, width):
-    for axis, dim in sides:
-        size, length = (lax.axis_size(axis), x.shape[dim])
-        up = [(i, (i + 1) % size) for i in range(size - 1)]
-        down = [(j, i) for i, j in up]
-        last = lax.slice_in_dim(x, length - width, length, axis=dim)
-        first = lax.slice_in_dim(x, 0, width, axis=dim)
-        before = lax.ppermute(last, axis, up)
-        after = lax.ppermute(first, axis, down)
-        x = jnp.concatenate([before, x, after], axis=dim)
-    return x
+NEAR = [(dr, dc) for dr in (-1, 0, 1) for dc in (-1, 0, 1) if (dr, dc) != (0, 0)]
+EDGE = 8
+
+
+def entry_kernel(
+    count, grid,
+    f_ref, cot_ref, edges_ref, taps_ref, f_out, gm_out, pad_out,
+    row_halo, col_halo, pad, gm_src, send, recv, near_send, near_recv,
+):
+    members, rows, cols, width = cot_ref.shape
+    me = lax.axis_index("mem")
+    at = (lax.axis_index("row"), lax.axis_index("col"))
+    others = [lax.rem(me + k, count) for k in range(1, count)]
+
+    def exists(step):
+        tests = [
+            (at[i] > 0) if step[i] < 0 else (at[i] < grid[i] - 1) for i in range(2) if step[i]
+        ]
+        return functools.reduce(jnp.logical_and, tests)
+
+    def neighbour(step):
+        return (me, at[0] + step[0], at[1] + step[1])
+
+    def outgoing(step):
+        dr, dc = step
+        if dc == 0:
+            return cot_ref.at[:, 0 if dr < 0 else rows - 1]
+        side = edges_ref.at[0 if dc < 0 else 1]
+        return side if dr == 0 else side.at[0 if dr < 0 else rows - 1]
+
+    def landing(step):
+        dr, dc = step
+        if dc == 0:
+            return row_halo.at[0 if dr < 0 else 1]
+        side = col_halo.at[0 if dc < 0 else 1]
+        return side.at[pl.ds(1, rows)] if dr == 0 else side.at[0 if dr < 0 else rows + 1]
+
+    def halo_copy(i):
+        step = NEAR[i]
+        back = len(NEAR) - 1 - i
+        return push(
+            outgoing(step), landing(NEAR[back]), near_send.at[i], near_recv.at[back],
+            neighbour(step),
+        )
+
+    barrier = pltpu.get_barrier_semaphore()
+    for o in others:
+        pl.semaphore_signal(barrier, inc=1, device_id=(o, *at), device_id_type=MESH)
+    for step in NEAR:
+        @pl.when(exists(step))
+        def _():
+            pl.semaphore_signal(barrier, inc=1, device_id=neighbour(step), device_id_type=MESH)
+    present = sum(exists(step).astype(jnp.int32) for step in NEAR)
+    pl.semaphore_wait(barrier, present + len(others))
+
+    for i in range(len(NEAR)):
+        @pl.when(exists(NEAR[i]))
+        def _():
+            halo_copy(i).start()
+
+        @pl.when(jnp.logical_not(exists(NEAR[i])))
+        def _():
+            there = landing(NEAR[i])
+            there[...] = jnp.zeros(there.shape, BF16)
+    srcs, dsts = (f_ref, gm_src), (f_out, gm_out)
+
+    def spread(t):
+        copies = []
+        for o in others:
+            copy = push(
+                srcs[t].at[:, o], dsts[t].at[me], send.at[t, o], recv.at[t, me], (o, *at)
+            )
+            copy.start()
+            copies.append(copy)
+        dsts[t][me] = srcs[t][:, me]
+        return copies
+
+    copies = spread(0)
+    pad[:, 1 : rows + 1, EDGE : EDGE + cols, :] = cot_ref[...].astype(F32)
+    for i in range(len(NEAR)):
+        @pl.when(exists(NEAR[i]))
+        def _():
+            there = landing(NEAR[i])
+            push(
+                there, there, near_send.at[i], near_recv.at[i], neighbour(NEAR[i])
+            ).wait_recv()
+    pad[:, 0, EDGE : EDGE + cols, :] = row_halo[0].astype(F32)
+    pad[:, rows + 1, EDGE : EDGE + cols, :] = row_halo[1].astype(F32)
+    for side, place in ((0, EDGE - 1), (1, EDGE + cols)):
+        for r in range(rows + 2):
+            column = col_halo[side, r].astype(F32)
+            for m in range(members):
+                pad[m, r, place : place + 1, :] = column[m : m + 1]
+    for m in range(members):
+        summed = jnp.zeros((rows, cols, width), F32)
+        for i in range(3):
+            for j in range(3):
+                first = EDGE + 1 - j
+                summed = summed + taps_ref[3 * i + j : 3 * i + j + 1, :] * pad[
+                    m, 2 - i : 2 - i + rows, first : first + cols, :
+                ]
+        gm_src[m] = summed.reshape(gm_src.shape[1:]).astype(BF16)
+    copies += spread(1)
+    pad_out[...] = pad[:, :, EDGE - 1 : EDGE + 1 + cols, :].astype(BF16)
+    for i in range(len(NEAR)):
+        @pl.when(exists(NEAR[i]))
+        def _():
+            halo_copy(i).wait_send()
+    for copy in copies:
+        copy.wait_send()
+    for t in range(2):
+        for o in others:
+            push(
+                srcs[t].at[:, o], dsts[t].at[o], send.at[t, o], recv.at[t, o], (o, *at)
+            ).wait_recv()
+
+
+def entry(fields, cotangent, taps, collective_id):
+    count = lax.axis_size("mem")
+    members, rows, cols, width = fields.shape
+    cells = rows * cols // count
+    split = (members, count, cells, width)
+    got = (count, members, cells, width)
+    edges = jnp.swapaxes(jnp.stack([cotangent[:, :, 0], cotangent[:, :, -1]]), 1, 2)
+    sems = pltpu.SemaphoreType.DMA
+    return pl.pallas_call(
+        functools.partial(entry_kernel, count, (lax.axis_size("row"), lax.axis_size("col"))),
+        out_shape=(
+            jax.ShapeDtypeStruct(got, BF16),
+            jax.ShapeDtypeStruct(got, BF16),
+            jax.ShapeDtypeStruct((members, rows + 2, cols + 2, width), BF16),
+        ),
+        in_specs=[VMEM_SPEC] * 4,
+        out_specs=(VMEM_SPEC,) * 3,
+        scratch_shapes=[
+            pltpu.VMEM((2, members, cols, width), BF16),
+            pltpu.VMEM((2, rows + 2, members, width), BF16),
+            pltpu.VMEM((members, rows + 2, cols + 2 * EDGE, width), F32),
+            pltpu.VMEM(split, BF16),
+            sems((2, count)), sems((2, count)), sems((len(NEAR),)), sems((len(NEAR),)),
+        ],
+        compiler_params=pltpu.CompilerParams(
+            collective_id=collective_id, has_side_effects=True, vmem_limit_bytes=48 * 2**20
+        ),
+    )(fields.reshape(split), cotangent, edges, taps)
 
 
 def local(fields, norm_gain, w_query, w_key, w_value, w_out, mix_kernel, cotangent):
     members, tile_rows, tile_cols, width = fields.shape
     cells = tile_rows * tile_cols
-    padded_cot = with_halo(cotangent, (("row", 1), ("col", 2)), 1)
+    count = lax.axis_size("mem")
+    f_got, gm_got, padded_cot = entry(fields, cotangent, mix_kernel.reshape(9, width), 1)
     shifts = [
         padded_cot[:, 2 - i : 2 - i + tile_rows, 2 - j : 2 - j + tile_cols, :].astype(F32)
         for i in range(3)
         for j in range(3)
     ]
-    taps = mix_kernel.reshape(9, width)
-    summed = jnp.zeros(fields.shape, F32)
-    for i in range(9):
-        summed = summed + taps[i] * shifts[i]
-    count = lax.axis_size("mem")
-    split = (members, count, cells // count, width)
-    f_got, gm_got = exchange(fields.reshape(split), summed.astype(BF16).reshape(split), True, 1)
     joined = (members * count, cells // count, width)
     corr, mixed, grads, gain = block(
         f_got.reshape(joined), gm_got.reshape(joined), norm_gain, w_query, w_key, w_value, w_out
     )
     sender = (count, members, cells // count, width)
-    corr, mixed = exchange(corr.reshape(sender), mixed.reshape(sender), False, 2)
+    corr, mixed = exchange(corr.reshape(sender), mixed.reshape(sender), 2)
     grad_fields = (cotangent.astype(F32) + corr.reshape(fields.shape).astype(F32)).astype(BF16)
     mixed = mixed.reshape(fields.shape).astype(F32)
     terms = [jnp.sum(s * mixed, axis=(0, 1, 2))[None] for s in shifts]

time: 84.5 us -> 66.4 us (0.79)
  starting transfers between devices: 12.1 us -> 0 us
  waiting for transfers between devices: 5.57 us -> 0 us
  other arithmetic: 3.92 us -> 2.3 us
  Pallas kernels: 53.8 us -> 55.3 us
    ppermute x4 -> x0, starting transfers between devices: 12.1 us -> none  [the longest x2 9.5 us: with_halo(): before = lax.ppermute(last, axis, up)]
    ppermute x4 -> x0, waiting for transfers between devices: 5.57 us -> none  [the longest x2 4.09 us: with_halo(): after = lax.ppermute(first, axis, down)]
    pallas_call x2, Pallas kernels: 19.8 us -> 22.6 us  [the longest x1 12.7 us: entry(): pl.pallas_call(functools.partial(entry_kernel, count, (lax.axis_size('row...]
    pallas_call x1, Pallas kernels: 24.3 us -> 23 us  [sum_all(): pl.pallas_call(functools.partial(sum_kernel, planes, rows, cols, scale),...]
    reduce_sum x1, other arithmetic: 2.49 us -> 1.5 us  [local(): terms = [jnp.sum(s * mixed, axis=(0, 1, 2))[None] for s in shifts]]
    unnamed x22 -> x24, local copies, waits for them, and re-layouts: 3.98 us -> 4.64 us
  transfers between devices with their start and end apart: 4 -> 0, of which waited for: 2 -> 0; matrix products, arithmetic and copies ran while one was open for 1% -> 0% of each run, Pallas kernels for 0% -> 0%
where the time goes in v3:
time: 66.4 us; the launch traced here: 66.1 us
  Pallas kernels  55.3 us (83%)
  local copies, waits for them, and re-layouts  7.77 us (12%)
  other arithmetic  2.3 us (3%)
  between operations  0.77 us (1%)
    pallas_call x1, Pallas kernels, sum_all(): pl.pallas_call(functools.partial(sum_kernel, planes, rows, cols, scale),...  23 us
    pallas_call x1, Pallas kernels, entry(): pl.pallas_call(functools.partial(entry_kernel, count, (lax.axis_size('row...  12.7 us
    pallas_call x1, Pallas kernels, exchange(): pl.pallas_call(functools.partial(exchange_kernel, count), out_shape=(jax....  9.87 us
    pallas_call x1, Pallas kernels, block(): pl.pallas_call(block_kernel, out_shape=(jax.ShapeDtypeStruct(f.shape, BF1...  9.69 us
    unnamed x24, local copies, waits for them, and re-layouts  4.64 us
    reduce_sum x1, other arithmetic, local(): terms = [jnp.sum(s * mixed, axis=(0, 1, 2))[None] for s in shifts]  1.5 us

profile of v3, /device:TPU:0, one launch (start us, length us, event | category | flops | bytes accessed | tf_op | source)
XLA Modules:
  0.0 66.1 jit_solution(14333057610613121114)
XLA Ops:
  0.6 0.9 %fusion.10 = (bf16[4,4,1,256]{3,2,1,0:T(2,128)(2,1)S(1)}, bf16[4,4,1,256]{3,2,1,0:T(2,128)(2,1)S(1)}) fusion(bf16[4,4,32,256]{3,2,1,0:T(8,128)(2,1)} %cot_ref.1), kind=kLoop, calls=%fused_computation.23 | loop fusion | bytes 32768 | tf_op jit(solution)/shard_map/slice | solution.py:461
  1.6 0.0 copy-start.11
  1.6 0.7 %copy-done.11 = f32[3,3,256]{2,1,0:T(4,128)S(1)} copy-done((f32[3,3,256]{2,1,0:T(4,128)S(1)}, f32[3,3,256]{2,1,0:T(4,128)}, u32[]{:S(2)}) %copy-start.11) | copy-done | bytes 9240
  2.3 0.0 copy-start
  2.3 0.9 %copy-done = bf16[4,4,32,256]{3,2,1,0:T(8,128)(2,1)S(1)} copy-done((bf16[4,4,32,256]{3,2,1,0:T(8,128)(2,1)S(1)}, bf16[4,4,32,256]{3,2,1,0:T(8,128)(2,1)}, u32[]{:S(2)}) %copy-start) | copy-done | bytes 262168
  3.2 0.0 copy-start.2
  3.2 0.9 %copy-done.2 = bf16[4,4,32,256]{3,2,1,0:T(8,128)(2,1)S(1)} copy-done((bf16[4,4,32,256]{3,2,1,0:T(8,128)(2,1)S(1)}, bf16[4,4,32,256]{3,2,1,0:T(8,128)(2,1)}, u32[]{:S(2)}) %copy-start.2) | copy-done | bytes 262168
  4.2 0.0 copy-start.5
  4.2 0.0 copy-start.6
  4.2 12.7 %shard_map.135 = (bf16[4,4,32,256]{3,2,1,0:T(8,128)(2,1)S(1)}, bf16[4,4,32,256]{3,2,1,0:T(8,128)(2,1)S(1)}, bf16[4,6,34,256]{3,2,1,0:T(8,128)(2,1)S(1)}) custom-call(bf16[4,4,32,256]{3,2,1,0:T(8,128)(2,1)S(1)} %copy-done.2, bf16[4,4,32,256]{3,2,1,0:T(8,128)(2,1)S(1)} %copy-done, bf16[2,4,4,256]{3,2,1,0:T(4,128)(2,1)S(1)} %maximum_bitcast_fusion.edges_ref, ...), custom_call_target="tpu_custom_call" | custom-call | tf_op jit(solution)/shard_map/pallas_call | solution.py:463
  16.9 0.0 copy-start.9
  16.9 0.0 copy-done.5
  16.9 0.0 copy-done.6
  16.9 0.0 copy-done.7
  16.9 0.0 copy-done.8
  17.0 0.6 copy-done.9
  17.6 9.7 %shard_map.136 = (bf16[16,32,256]{2,1,0:T(8,128)(2,1)S(1)}, bf16[16,32,256]{2,1,0:T(8,128)(2,1)S(1)}, f32[1024,256]{1,0:T(8,128)S(1)}, f32[1,256]{1,0:T(1,128)S(1)}) custom-call(bf16[16,32,256]{2,1,0:T(8,128)(2,1)S(1)} %bitcast.25, bf16[16,32,256]{2,1,0:T(8,128)(2,1)S(1)} %bitcast.26, f32[1,256]{1,0:T(1,128)S(1)} %bitcast.29, ...), custom_call_target="tpu_custom_call" | custom-call | tf_op jit(solution)/shard_map/pallas_call | solution.py:120
  27.3 0.0 copy-start.3
  27.3 0.7 %copy-done.3 = bf16[16,32,256]{2,1,0:T(8,128)(2,1)} copy-done((bf16[16,32,256]{2,1,0:T(8,128)(2,1)}, bf16[16,32,256]{2,1,0:T(8,128)(2,1)S(1)}, u32[]{:S(2)}) %copy-start.3) | copy-done | bytes 262168
  28.0 0.7 %copy-done.4 = bf16[16,32,256]{2,1,0:T(8,128)(2,1)} copy-done((bf16[16,32,256]{2,1,0:T(8,128)(2,1)}, bf16[16,32,256]{2,1,0:T(8,128)(2,1)S(1)}, u32[]{:S(2)}) %copy-start.4) | copy-done | bytes 262168
  28.7 9.9 %shard_map.137 = (bf16[4,4,32,256]{3,2,1,0:T(8,128)(2,1)}, bf16[4,4,32,256]{3,2,1,0:T(8,128)(2,1)}) custom-call(bf16[4,4,32,256]{3,2,1,0:T(8,128)(2,1)} %bitcast.27, bf16[4,4,32,256]{3,2,1,0:T(8,128)(2,1)} %bitcast.28), custom_call_target="tpu_custom_call" | custom-call | tf_op jit(solution)/shard_map/pallas_call | solution.py:190
  38.6 1.5 %fusion.8 = (f32[256]{0:T(256)S(1)}, f32[256]{0:T(256)S(1)}, f32[256]{0:T(256)S(1)}, f32[256]{0:T(256)S(1)}, f32[256]{0:T(256)S(1)}, /*index=5*/f32[256]{0:T(256...) fusion(bf16[4,4,32,256]{3,2,1,0:T(8,128)(2,1)} %get-tuple-element.26, bf16[4,6,34,256]{3,2,1,0:T(8,128)(2,1)S(1)} %get-tuple-element.25), kind=kLoop, calls=%fused_computation.17 | loop fusion | flops 3667712 | bytes 2630656 | tf_op jit(solution)/shard_map/reduce_sum | solution.py:503
  40.1 0.1 concatenate.3.s_ref
  40.1 23.0 %shard_map.138 = (f32[2,4,4,32,256]{4,3,2,1,0:T(8,128)S(1)}, f32[16,256]{1,0:T(8,128)S(1)}) custom-call(f32[2,4,4,32,256]{4,3,2,1,0:T(8,128)S(1)} %bitcast.23, f32[16,256]{1,0:T(8,128)S(1)} %concatenate.3.s_ref), custom_call_target="tpu_custom_call" | custom-call | tf_op jit(solution)/shard_map/pallas_call | solution.py:314
  63.1 0.0 copy-start.1
  63.1 0.0 copy-start.10
  63.1 1.0 %fusion.9 = (f32[256,256]{1,0:T(8,128)}, f32[256,256]{1,0:T(8,128)}, f32[256,256]{1,0:T(8,128)}, f32[256,256]{1,0:T(8,128)}) fusion(f32[1024,256]{1,0:T(8,128)S(1)} %bitcast.24), kind=kLoop, calls=%fused_computation.22 | loop fusion | bytes 2097152 | tf_op jit(solution)/shard_map/slice | solution.py:509
  64.1 0.6 reshape.49
  64.7 0.6 slice.62
  65.3 0.0 copy-done.1
  65.3 0.0 copy-done.10
  65.3 0.8 %add_convert_fusion = bf16[4,4,32,256]{3,2,1,0:T(8,128)(2,1)} fusion(bf16[4,4,32,256]{3,2,1,0:T(8,128)(2,1)S(1)} %copy-done.10, bf16[4,4,32,256]{3,2,1,0:T(8,128)(2,1)S(1)} %copy-done.1), kind=kLoop, calls=%fused_computation.18 | loop fusion | flops 524288 | bytes 786432 | tf_op jit(solution)/shard_map/convert_element_type | solution.py:501
  (8 shorter events, 0.0 us)
Async XLA Ops:
  1.6 0.7 %copy-start.11 = (f32[3,3,256]{2,1,0:T(4,128)S(1)}, f32[3,3,256]{2,1,0:T(4,128)}, u32[]{:S(2)}) copy-start(f32[3,3,256]{2,1,0:T(4,128)} %param.14) | copy-start | bytes 27652
  2.3 0.9 %copy-start = (bf16[4,4,32,256]{3,2,1,0:T(8,128)(2,1)S(1)}, bf16[4,4,32,256]{3,2,1,0:T(8,128)(2,1)}, u32[]{:S(2)}) copy-start(bf16[4,4,32,256]{3,2,1,0:T(8,128)(2,1)} %cot_ref.1) | copy-start | bytes 786436
  3.2 0.9 %copy-start.2 = (bf16[4,4,32,256]{3,2,1,0:T(8,128)(2,1)S(1)}, bf16[4,4,32,256]{3,2,1,0:T(8,128)(2,1)}, u32[]{:S(2)}) copy-start(bf16[4,4,32,256]{3,2,1,0:T(8,128)(2,1)} %f_ref.1) | copy-start | bytes 786436
  4.2 12.7 %copy-start.5 = (bf16[256,256]{1,0:T(8,128)(2,1)S(1)}, bf16[256,256]{1,0:T(8,128)(2,1)}, u32[]{:S(2)}) copy-start(bf16[256,256]{1,0:T(8,128)(2,1)} %wq_ref.1) | copy-start | bytes 393220
  4.2 12.7 %copy-start.6 = (bf16[256,256]{1,0:T(8,128)(2,1)S(1)}, bf16[256,256]{1,0:T(8,128)(2,1)}, u32[]{:S(2)}) copy-start(bf16[256,256]{1,0:T(8,128)(2,1)} %wk_ref.1) | copy-start | bytes 393220
  4.2 12.8 %copy-start.7 = (bf16[256,256]{1,0:T(8,128)(2,1)S(1)}, bf16[256,256]{1,0:T(8,128)(2,1)}, u32[]{:S(2)}) copy-start(bf16[256,256]{1,0:T(8,128)(2,1)} %wv_ref.1) | copy-start | bytes 393220
  4.2 12.8 %copy-start.8 = (bf16[256,256]{1,0:T(8,128)(2,1)S(1)}, bf16[256,256]{1,0:T(8,128)(2,1)}, u32[]{:S(2)}) copy-start(bf16[256,256]{1,0:T(8,128)(2,1)} %wo_ref.1) | copy-start | bytes 393220
  16.9 0.7 %copy-start.9 = (f32[256]{0:T(256)S(1)}, f32[256]{0:T(256)}, u32[]{:S(2)}) copy-start(f32[256]{0:T(256)} %param.9) | copy-start | bytes 3076
  27.3 0.7 %copy-start.3 = (bf16[16,32,256]{2,1,0:T(8,128)(2,1)}, bf16[16,32,256]{2,1,0:T(8,128)(2,1)S(1)}, u32[]{:S(2)}) copy-start(bf16[16,32,256]{2,1,0:T(8,128)(2,1)S(1)} %get-tuple-element.20) | copy-start | bytes 786436
  28.0 0.7 %copy-start.4 = (bf16[16,32,256]{2,1,0:T(8,128)(2,1)}, bf16[16,32,256]{2,1,0:T(8,128)(2,1)S(1)}, u32[]{:S(2)}) copy-start(bf16[16,32,256]{2,1,0:T(8,128)(2,1)S(1)} %get-tuple-element.21) | copy-start | bytes 786436
  63.1 2.2 %copy-start.1 = (bf16[4,4,32,256]{3,2,1,0:T(8,128)(2,1)S(1)}, bf16[4,4,32,256]{3,2,1,0:T(8,128)(2,1)}, u32[]{:S(2)}) copy-start(bf16[4,4,32,256]{3,2,1,0:T(8,128)(2,1)} %cot_ref.1) | copy-start | bytes 786436
  63.1 2.2 %copy-start.10 = (bf16[4,4,32,256]{3,2,1,0:T(8,128)(2,1)S(1)}, bf16[4,4,32,256]{3,2,1,0:T(8,128)(2,1)}, u32[]{:S(2)}) copy-start(bf16[4,4,32,256]{3,2,1,0:T(8,128)(2,1)} %get-tuple-element.22) | copy-start | bytes 786436

commit v4 on v3

--- a/solution.py
+++ b/solution.py
@@ -148,62 +148,55 @@
     )
 
 
-def exchange_kernel(count, *refs):
-    inward = False
-    srcs, dsts, (send, recv) = refs[:2], refs[2:4], refs[4:]
+def exchange_kernel(count, src, dst, send, recv):
     me = lax.axis_index("mem")
     row, col = lax.axis_index("row"), lax.axis_index("col")
     others = [lax.rem(me + k, count) for k in range(1, count)]
     enter([(o, row, col) for o in others])
 
-    def view(ref, i, by_chunk):
-        return ref.at[:, i] if by_chunk else ref.at[i]
-
-    copies = []
-    for t in range(2):
-        for o in others:
-            copy = push(
-                view(srcs[t], o, inward), view(dsts[t], me, not inward),
-                send.at[t, o], recv.at[t, me], (o, row, col),
-            )
-            copy.start()
-            copies.append(copy)
-    for t in range(2):
-        if inward:
-            dsts[t][me] = srcs[t][:, me]
-        else:
-            dsts[t][:, me] = srcs[t][me]
+    copies, arrivals = exchange_start(src, dst, send, recv, me, others, (row, col))
+    exchange_finish(copies, arrivals)
+
+
+def exchange_start(src, dst, send, recv, me, others, place):
+    copies, arrivals = [], []
+    for o in others:
+        copy = push(src.at[o], dst.at[:, me], send.at[o], recv.at[me], (o, *place))
+        copy.start()
+        copies.append(copy)
+        arrivals.append(push(src.at[o], dst.at[:, o], send.at[o], recv.at[o], (o, *place)))
+    dst[:, me] = src[me]
+    return copies, arrivals
+
+
+def exchange_finish(copies, arrivals):
     for copy in copies:
         copy.wait_send()
-    for t in range(2):
-        for o in others:
-            push(
-                view(srcs[t], o, inward), view(dsts[t], o, not inward),
-                send.at[t, o], recv.at[t, o], (o, row, col),
-            ).wait_recv()
-
-
-def exchange(a, b, collective_id):
+    for arrival in arrivals:
+        arrival.wait_recv()
+
+
+def exchange(a, collective_id):
     count = lax.axis_size("mem")
     shape = a.shape
     out = (shape[1], shape[0]) + shape[2:]
     return pl.pallas_call(
         functools.partial(exchange_kernel, count),
-        out_shape=(jax.ShapeDtypeStruct(out, a.dtype),) * 2,
-        in_specs=[VMEM_SPEC] * 2,
-        out_specs=(VMEM_SPEC,) * 2,
-        scratch_shapes=[pltpu.SemaphoreType.DMA((2, count))] * 2,
+        out_shape=jax.ShapeDtypeStruct(out, a.dtype),
+        in_specs=[VMEM_SPEC],
+        out_specs=VMEM_SPEC,
+        scratch_shapes=[pltpu.SemaphoreType.DMA((count,))] * 2,
         compiler_params=pltpu.CompilerParams(collective_id=collective_id, has_side_effects=True),
-    )(a, b)
+    )(a)
 
 
 def sum_kernel(
-    planes, rows, cols, scale,
-    g_ref, s_ref, out_ref, sout_ref,
+    count, planes, rows, cols, scale,
+    g_ref, s_ref, x_ref, out_ref, sout_ref, x_out,
     a_src, a_dst, acc1, b_src, b_dst, acc2, c_src, c_dst, gz, gp, ga, s_a, s_b, s_c,
     send_a, recv_a, send_b, recv_b, send_c, recv_c,
     send_z, recv_z, send_p, recv_p, send_g, recv_g,
-    ssend_b, srecv_b, ssend_c, srecv_c, ssend_a, srecv_a,
+    ssend_b, srecv_b, ssend_c, srecv_c, ssend_a, srecv_a, xsend, xrecv,
 ):
     mem, row, col = (lax.axis_index(a) for a in ("mem", "row", "col"))
     core = lax.rem(mem, 2)
@@ -216,8 +209,10 @@
 
     plane_others = [lax.rem(me_p + k, planes) for k in range(1, planes)]
     row_others = [lax.rem(row + k, rows) for k in range(1, rows)]
+    mem_others = [lax.rem(mem + k, count) for k in range(1, count)]
     enter(
-        [partner]
+        [(o, row, col) for o in mem_others]
+        + [partner]
         + [plane_peer(p) for p in plane_others]
         + [(mem, r, col) for r in row_others]
     )
@@ -228,6 +223,7 @@
     s_a[core] = s_ref[...]
     small = push(s_a.at[core], s_a.at[core], ssend_a, srecv_a, partner)
     small.start()
+    moving = exchange_start(x_ref, x_out, xsend, xrecv, mem, mem_others, (row, col))
     first.wait()
     acc1[...] = g_ref[core] + a_dst[...].astype(F32)
     b_src[...] = acc1[...].astype(BF16)
@@ -301,9 +297,12 @@
         out_ref[other, p] = ga[p].astype(F32)
     for copy in sent:
         copy.wait_send()
-
-
-def sum_all(grads, small, scale, collective_id):
+    exchange_finish(*moving)
+
+
+def sum_all(grads, small, x, scale, collective_id):
+    count = lax.axis_size("mem")
+    x_shape = (x.shape[1], x.shape[0]) + x.shape[2:]
     rows, cols = lax.axis_size("row"), lax.axis_size("col")
     planes = lax.axis_size("mem") // 2 * cols
     height, width = grads.shape
@@ -311,11 +310,15 @@
     part, half = (rows,) + unit, (planes, rows) + unit
     full = (2,) + half
     sems = pltpu.SemaphoreType.DMA
-    out, sout = pl.pallas_call(
-        functools.partial(sum_kernel, planes, rows, cols, scale),
-        out_shape=(jax.ShapeDtypeStruct(full, F32), jax.ShapeDtypeStruct(small.shape, F32)),
-        in_specs=[VMEM_SPEC] * 2,
-        out_specs=(VMEM_SPEC,) * 2,
+    out, sout, x = pl.pallas_call(
+        functools.partial(sum_kernel, count, planes, rows, cols, scale),
+        out_shape=(
+            jax.ShapeDtypeStruct(full, F32),
+            jax.ShapeDtypeStruct(small.shape, F32),
+            jax.ShapeDtypeStruct(x_shape, x.dtype),
+        ),
+        in_specs=[VMEM_SPEC] * 3,
+        out_specs=(VMEM_SPEC,) * 3,
         scratch_shapes=[
             pltpu.VMEM(half, BF16), pltpu.VMEM(half, BF16), pltpu.VMEM(half, F32),
             pltpu.VMEM(half, BF16), pltpu.VMEM(half, BF16), pltpu.VMEM(part, F32),
@@ -328,12 +331,13 @@
             sems((rows,)), sems((rows,)), sems((planes,)), sems((planes,)),
             sems((planes,)), sems((planes,)),
             sems((planes,)), sems((planes,)), sems((rows,)), sems((rows,)), sems(()), sems(()),
+            sems((count,)), sems((count,)),
         ],
         compiler_params=pltpu.CompilerParams(
             collective_id=collective_id, has_side_effects=True, vmem_limit_bytes=48 * 2**20
         ),
-    )(grads.reshape(full), small)
-    return out.reshape(height, width), sout
+    )(grads.reshape(full), small, x)
+    return out.reshape(height, width), sout, x
 
 NEAR = [(dr, dc) for dr in (-1, 0, 1) for dc in (-1, 0, 1) if (dr, dc) != (0, 0)]
 EDGE = 8
@@ -497,15 +501,15 @@
         f_got.reshape(joined), gm_got.reshape(joined), norm_gain, w_query, w_key, w_value, w_out
     )
     sender = (count, members, cells // count, width)
-    corr, mixed = exchange(corr.reshape(sender), mixed.reshape(sender), 2)
-    grad_fields = (cotangent.astype(F32) + corr.reshape(fields.shape).astype(F32)).astype(BF16)
+    mixed = exchange(mixed.reshape(sender), 2)
     mixed = mixed.reshape(fields.shape).astype(F32)
     terms = [jnp.sum(s * mixed, axis=(0, 1, 2))[None] for s in shifts]
     small = jnp.concatenate([gain, *terms, jnp.zeros((6, width), F32)])
     tokens = math.prod(fields.shape[:3]) * math.prod(
         lax.axis_size(a) for a in ("mem", "row", "col")
     )
-    total, small = sum_all(grads, small, 1.0 / math.sqrt(tokens), 3)
+    total, small, corr = sum_all(grads, small, corr.reshape(sender), 1.0 / math.sqrt(tokens), 3)
+    grad_fields = (cotangent.astype(F32) + corr.reshape(fields.shape).astype(F32)).astype(BF16)
     w = [total[i * width : (i + 1) * width] for i in range(4)]
     return (grad_fields, small[0], *w, small[1:10].reshape(3, 3, width))
 

time: 66.4 us -> 64.5 us (0.971)
  Pallas kernels: 55.3 us -> 54 us
  local copies, waits for them, and re-layouts: 7.77 us -> 7.08 us
    unnamed x24 -> x18, local copies, waits for them, and re-layouts: 4.64 us -> 3.24 us
    pallas_call x2, Pallas kernels: 32.9 us -> 31.6 us  [the longest x1 24.8 us: sum_all(): pl.pallas_call(functools.partial(sum_kernel, count, planes, rows, cols, s...]
    reshape x1, local copies, waits for them, and re-layouts: 0.01 us -> 0.72 us  [local(): mix_kernel.reshape(9, width)]
where the time goes in v4:
time: 64.5 us; the launch traced here: 64.2 us
  Pallas kernels  54 us (84%)
  local copies, waits for them, and re-layouts  7.08 us (11%)
  other arithmetic  2.3 us (4%)
  between operations  0.76 us (1%)
    pallas_call x1, Pallas kernels, sum_all(): pl.pallas_call(functools.partial(sum_kernel, count, planes, rows, cols, s...  24.8 us
    pallas_call x1, Pallas kernels, entry(): pl.pallas_call(functools.partial(entry_kernel, count, (lax.axis_size('row...  12.7 us
    pallas_call x1, Pallas kernels, block(): pl.pallas_call(block_kernel, out_shape=(jax.ShapeDtypeStruct(f.shape, BF1...  9.69 us
    pallas_call x1, Pallas kernels, exchange(): pl.pallas_call(functools.partial(exchange_kernel, count), out_shape=jax.S...  6.8 us
    unnamed x18, local copies, waits for them, and re-layouts  3.24 us
    reduce_sum x1, other arithmetic, local(): terms = [jnp.sum(s * mixed, axis=(0, 1, 2))[None] for s in shifts]  1.5 us

profile of v4, /device:TPU:0, one launch (start us, length us, event | category | flops | bytes accessed | tf_op | source)
XLA Modules:
  0.0 64.2 jit_solution(13598561301301055667)
XLA Ops:
  0.6 0.7 %reshape.41.taps_ref = f32[9,256]{1,0:T(8,128)S(1)} reshape(f32[3,3,256]{2,1,0:T(4,128)} %param.14) | data formatting | bytes 18432 | tf_op jit(solution)/shard_map/reshape | solution.py:493
  1.3 0.9 %fusion.10 = (bf16[4,4,1,256]{3,2,1,0:T(2,128)(2,1)S(1)}, bf16[4,4,1,256]{3,2,1,0:T(2,128)(2,1)S(1)}) fusion(bf16[4,4,32,256]{3,2,1,0:T(8,128)(2,1)} %cot_ref.1), kind=kLoop, calls=%fused_computation.23 | loop fusion | bytes 32768 | tf_op jit(solution)/shard_map/slice | solution.py:465
  2.3 0.0 copy-start
  2.3 0.9 %copy-done = bf16[4,4,32,256]{3,2,1,0:T(8,128)(2,1)S(1)} copy-done((bf16[4,4,32,256]{3,2,1,0:T(8,128)(2,1)S(1)}, bf16[4,4,32,256]{3,2,1,0:T(8,128)(2,1)}, u32[]{:S(2)}) %copy-start) | copy-done | bytes 262168
  3.2 0.0 copy-start.2
  3.3 0.9 %copy-done.2 = bf16[4,4,32,256]{3,2,1,0:T(8,128)(2,1)S(1)} copy-done((bf16[4,4,32,256]{3,2,1,0:T(8,128)(2,1)S(1)}, bf16[4,4,32,256]{3,2,1,0:T(8,128)(2,1)}, u32[]{:S(2)}) %copy-start.2) | copy-done | bytes 262168
  4.2 0.0 copy-start.4
  4.2 0.0 copy-start.5
  4.2 0.0 copy-start.6
  4.2 0.0 copy-start.7
  4.2 12.7 %shard_map.135 = (bf16[4,4,32,256]{3,2,1,0:T(8,128)(2,1)S(1)}, bf16[4,4,32,256]{3,2,1,0:T(8,128)(2,1)S(1)}, bf16[4,6,34,256]{3,2,1,0:T(8,128)(2,1)S(1)}) custom-call(bf16[4,4,32,256]{3,2,1,0:T(8,128)(2,1)S(1)} %copy-done.2, bf16[4,4,32,256]{3,2,1,0:T(8,128)(2,1)S(1)} %copy-done, bf16[2,4,4,256]{3,2,1,0:T(4,128)(2,1)S(1)} %maximum_bitcast_fusion.edges_ref, ...), custom_call_target="tpu_custom_call" | custom-call | tf_op jit(solution)/shard_map/pallas_call | solution.py:467
  16.9 0.0 copy-start.8
  16.9 0.0 copy-done.4
  16.9 0.0 copy-done.5
  17.0 0.0 copy-done.6
  17.0 0.0 copy-done.7
  17.0 0.6 copy-done.8
  17.6 9.7 %shard_map.136 = (bf16[16,32,256]{2,1,0:T(8,128)(2,1)S(1)}, bf16[16,32,256]{2,1,0:T(8,128)(2,1)S(1)}, f32[1024,256]{1,0:T(8,128)S(1)}, f32[1,256]{1,0:T(1,128)S(1)}) custom-call(bf16[16,32,256]{2,1,0:T(8,128)(2,1)S(1)} %bitcast.25, bf16[16,32,256]{2,1,0:T(8,128)(2,1)S(1)} %bitcast.26, f32[1,256]{1,0:T(1,128)S(1)} %bitcast.29, ...), custom_call_target="tpu_custom_call" | custom-call | tf_op jit(solution)/shard_map/pallas_call | solution.py:120
  27.3 0.0 copy-start.3
  27.3 0.7 %copy-done.3 = bf16[16,32,256]{2,1,0:T(8,128)(2,1)} copy-done((bf16[16,32,256]{2,1,0:T(8,128)(2,1)}, bf16[16,32,256]{2,1,0:T(8,128)(2,1)S(1)}, u32[]{:S(2)}) %copy-start.3) | copy-done | bytes 262168
  28.0 6.8 %shard_map.137 = bf16[4,4,32,256]{3,2,1,0:T(8,128)(2,1)} custom-call(bf16[4,4,32,256]{3,2,1,0:T(8,128)(2,1)} %bitcast.27), custom_call_target="tpu_custom_call" | custom-call | tf_op jit(solution)/shard_map/pallas_call | solution.py:183
  34.8 1.5 %fusion.8 = (f32[256]{0:T(256)S(1)}, f32[256]{0:T(256)S(1)}, f32[256]{0:T(256)S(1)}, f32[256]{0:T(256)S(1)}, f32[256]{0:T(256)S(1)}, /*index=5*/f32[256]{0:T(256...) fusion(bf16[4,4,32,256]{3,2,1,0:T(8,128)(2,1)} %shard_map.137, bf16[4,6,34,256]{3,2,1,0:T(8,128)(2,1)S(1)} %get-tuple-element.21), kind=kLoop, calls=%fused_computation.17 | loop fusion | flops 3667712 | bytes 2630656 | tf_op jit(solution)/shard_map/reduce_sum | solution.py:506
  36.3 0.1 concatenate.3.s_ref
  36.4 0.0 copy-start.1
  36.4 24.8 %shard_map.138 = (f32[2,4,4,32,256]{4,3,2,1,0:T(8,128)S(1)}, f32[16,256]{1,0:T(8,128)S(1)}, bf16[4,4,32,256]{3,2,1,0:T(8,128)(2,1)S(1)}) custom-call(f32[2,4,4,32,256]{4,3,2,1,0:T(8,128)S(1)} %bitcast.23, f32[16,256]{1,0:T(8,128)S(1)} %concatenate.3.s_ref, bf16[4,4,32,256]{3,2,1,0:T(8,128)(2,1)S(1)} %bitcast.28), custom_call_target="tpu_custom_call" | custom-call | tf_op jit(solution)/shard_map/pallas_call | solution.py:313
  61.2 0.0 copy-done.1
  61.2 0.8 %add_convert_fusion = bf16[4,4,32,256]{3,2,1,0:T(8,128)(2,1)} fusion(bf16[4,4,32,256]{3,2,1,0:T(8,128)(2,1)S(1)} %get-tuple-element.24, bf16[4,4,32,256]{3,2,1,0:T(8,128)(2,1)S(1)} %copy-done.1), kind=kLoop, calls=%fused_computation.18 | loop fusion | flops 524288 | bytes 786432 | tf_op jit(solution)/shard_map/convert_element_type | solution.py:512
  62.0 1.0 %fusion.9 = (f32[256,256]{1,0:T(8,128)}, f32[256,256]{1,0:T(8,128)}, f32[256,256]{1,0:T(8,128)}, f32[256,256]{1,0:T(8,128)}) fusion(f32[1024,256]{1,0:T(8,128)S(1)} %bitcast.24), kind=kLoop, calls=%fused_computation.22 | loop fusion | bytes 2097152 | tf_op jit(solution)/shard_map/slice | solution.py:513
  63.0 0.6 slice.62
  63.6 0.6 reshape.49
  (4 shorter events, 0.0 us)
Async XLA Ops:
  2.3 1.0 %copy-start = (bf16[4,4,32,256]{3,2,1,0:T(8,128)(2,1)S(1)}, bf16[4,4,32,256]{3,2,1,0:T(8,128)(2,1)}, u32[]{:S(2)}) copy-start(bf16[4,4,32,256]{3,2,1,0:T(8,128)(2,1)} %cot_ref.1) | copy-start | bytes 786436
  3.2 0.9 %copy-start.2 = (bf16[4,4,32,256]{3,2,1,0:T(8,128)(2,1)S(1)}, bf16[4,4,32,256]{3,2,1,0:T(8,128)(2,1)}, u32[]{:S(2)}) copy-start(bf16[4,4,32,256]{3,2,1,0:T(8,128)(2,1)} %f_ref.1) | copy-start | bytes 786436
  4.2 12.7 %copy-start.4 = (bf16[256,256]{1,0:T(8,128)(2,1)S(1)}, bf16[256,256]{1,0:T(8,128)(2,1)}, u32[]{:S(2)}) copy-start(bf16[256,256]{1,0:T(8,128)(2,1)} %wq_ref.1) | copy-start | bytes 393220
  4.2 12.7 %copy-start.5 = (bf16[256,256]{1,0:T(8,128)(2,1)S(1)}, bf16[256,256]{1,0:T(8,128)(2,1)}, u32[]{:S(2)}) copy-start(bf16[256,256]{1,0:T(8,128)(2,1)} %wk_ref.1) | copy-start | bytes 393220
  4.2 12.8 %copy-start.6 = (bf16[256,256]{1,0:T(8,128)(2,1)S(1)}, bf16[256,256]{1,0:T(8,128)(2,1)}, u32[]{:S(2)}) copy-start(bf16[256,256]{1,0:T(8,128)(2,1)} %wv_ref.1) | copy-start | bytes 393220
  4.2 12.8 %copy-start.7 = (bf16[256,256]{1,0:T(8,128)(2,1)S(1)}, bf16[256,256]{1,0:T(8,128)(2,1)}, u32[]{:S(2)}) copy-start(bf16[256,256]{1,0:T(8,128)(2,1)} %wo_ref.1) | copy-start | bytes 393220
  16.9 0.7 %copy-start.8 = (f32[256]{0:T(256)S(1)}, f32[256]{0:T(256)}, u32[]{:S(2)}) copy-start(f32[256]{0:T(256)} %param.9) | copy-start | bytes 3076
  27.3 0.7 %copy-start.3 = (bf16[16,32,256]{2,1,0:T(8,128)(2,1)}, bf16[16,32,256]{2,1,0:T(8,128)(2,1)S(1)}, u32[]{:S(2)}) copy-start(bf16[16,32,256]{2,1,0:T(8,128)(2,1)S(1)} %get-tuple-element.22) | copy-start | bytes 786436
  36.4 24.8 %copy-start.1 = (bf16[4,4,32,256]{3,2,1,0:T(8,128)(2,1)S(1)}, bf16[4,4,32,256]{3,2,1,0:T(8,128)(2,1)}, u32[]{:S(2)}) copy-start(bf16[4,4,32,256]{3,2,1,0:T(8,128)(2,1)} %cot_ref.1) | copy-start | bytes 786436
